TPU v7x, 512 devices: a whole 4x4x16 slice. The times are simulated.
512 devices in a mesh: slab: 128 (over z_hi, x, y, core), cell: 4 (over z_lo).
Axes of the slice: x: 4, y: 4, z: 16 (z_hi: 4, z_lo: 4; z = z_hi * 4 + z_lo), core: 2. Of those that a mesh axis runs over, the one named last changes fastest.
Arguments:
- charges: float32 [8, 128, 2048], P(None, 'slab', 'cell'), may hold values from -6 to 6
- counts: int32 [128, 2048], P('slab', 'cell'), may hold values from 1 to 8
- projection: float32 [8, 64, 128, 2048], P(None, None, 'slab', 'cell'), may hold values from -1.2 to 1.2
- near_blocks: float32 [6, 8, 8, 128, 2048], P(None, None, None, 'slab', 'cell'), may hold values from -0.9 to 0.9
- neighbours: int32 [6, 128, 2048], P(None, 'slab', 'cell'), may hold values from 0 to 26, as said below
- spectrum: float32 [512, 64, 512], P(None, None, 'slab'), may hold values from 0.25 to 4, as said below
Outputs:
- potentials: float32 [8, 128, 2048], P(None, 'slab', 'cell')
Inputs may be any that keep to these rules, and one draw needn't show every extreme that they name: `counts`: 8 is reached. neighbours[k, x, c] codes an offset in the 3 x 3 x 3 block of cells around c as in the near_field step; entry k = 0 is 13, the cell itself, and the 6 entries of a cell are distinct. spectrum[kx, kz, ky] = spectrum[(-kx) mod 512, (-kz) mod 64, (-ky) mod 512].
All inputs are finite; a program needn't handle non-finite values.
Results may differ from a plain program's by a relative error of at most 0.00005.
Values sent between devices are 32-bit elements; how exact they have to be, the bound alone decides.
A program may use at most 64 MiB of HBM per device.

v0:
```python
import math

import jax
import jax.numpy as jnp
from jax import lax
from jax.sharding import PartitionSpec as P

NX = 512
NY = 512
NZ = 64
TX = 4
TY = 4
TZ = 4
NZC = 16


def padded(value, sides, width):
    for axis, dim in sides:
        count, length = (lax.axis_size(axis), value.shape[dim])
        up = [(i, (i + 1) % count) for i in range(count)]
        down = [(j, i) for i, j in up]
        last = lax.slice_in_dim(value, length - width, length, axis=dim)
        first = lax.slice_in_dim(value, 0, width, axis=dim)
        before = lax.ppermute(last, axis, up)
        after = lax.ppermute(first, axis, down)
        value = jnp.concatenate([before, value, after], axis=dim)
    return value


def wave_tables(row_count, col_count, length):
    products = (
        lax.broadcasted_iota(jnp.int32, (row_count, col_count), 0)
        * lax.broadcasted_iota(jnp.int32, (row_count, col_count), 1)
        % length
    )
    angle_rad = products.astype(jnp.float32) * (2.0 * math.pi / length)
    return (jnp.cos(angle_rad), jnp.sin(angle_rad))


def depth_rows(freq_ids, valid, weights):
    depth_ids = lax.broadcasted_iota(jnp.int32, (freq_ids.shape[0], NZ), 1)
    products = freq_ids[:, None] * depth_ids % NZ
    angle_rad = products.astype(jnp.float32) * (2.0 * math.pi / NZ)
    basis = jnp.stack([jnp.cos(angle_rad), -jnp.sin(angle_rad)])
    return (basis * valid[None, :, None], basis * weights[None, :, None])


def full_depth_tables():
    freq_ids = lax.broadcasted_iota(jnp.int32, (NZ,), 0)
    ones = jnp.ones((NZ,), jnp.float32)
    forward_table, backward_table = depth_rows(freq_ids, ones, ones)
    return (forward_table, backward_table, freq_ids)


def combine_halves(first_part, second, orient):
    half_width = first_part.shape[-1] // 2
    real_part = first_part[..., :half_width] + orient * second[..., half_width:]
    imag_part = first_part[..., half_width:] - orient * second[..., :half_width]
    return jnp.concatenate([real_part, imag_part], axis=-1)


def transform_axis(pattern, cosine, sine_tab, values, orient):
    first_part = jnp.einsum(pattern, cosine, values, precision=lax.Precision.HIGHEST)
    second = jnp.einsum(pattern, sine_tab, values, precision=lax.Precision.HIGHEST)
    return combine_halves(first_part, second, orient)


def twiddle(values, twist_cos, twist_sin, orient):
    half_width = values.shape[-1] // 2
    real_part = values[..., :half_width]
    imag_part = values[..., half_width:]
    new_real = real_part * twist_cos + orient * imag_part * twist_sin
    new_imag = imag_part * twist_cos - orient * real_part * twist_sin
    return jnp.concatenate([new_real, new_imag], axis=-1)


def transform_rows(planes_block, cosine, sine_tab, orient):
    flat_rows = planes_block.reshape(-1, planes_block.shape[-1])
    first_part = jnp.dot(flat_rows, cosine, precision=lax.Precision.HIGHEST).reshape(
        planes_block.shape
    )
    second = jnp.dot(flat_rows, sine_tab, precision=lax.Precision.HIGHEST).reshape(
        planes_block.shape
    )
    real_part = first_part[:, 0] + orient * second[:, 1]
    imag_part = first_part[:, 1] - orient * second[:, 0]
    return jnp.stack([real_part, imag_part], axis=1)


def per_device(charges, counts, projection, near_blocks, neighbours, spectrum):
    panels, cell_planes, cell_cols = charges.shape
    planes = cell_planes * TX
    rows_cell = cell_cols // NZC
    slot_ids = lax.broadcasted_iota(jnp.int32, charges.shape, 0)
    panel_mask = (slot_ids < counts[None]).astype(jnp.float32)
    masked = charges * panel_mask
    tile_values = jnp.einsum("ptxc,pxc->txc", projection, masked, precision=lax.Precision.HIGHEST)
    grid_field = (
        tile_values.reshape(TX, TY, TZ, cell_planes, rows_cell, NZC)
        .transpose(3, 0, 5, 2, 4, 1)
        .reshape(planes, NZ, rows_cell * TY)
    )
    cell_count = lax.axis_size("cell")
    forward_table, backward_table, freq_ids = full_depth_tables()
    depth_count = forward_table.shape[1] // cell_count
    spectra_z = jnp.einsum(
        "wkz,xzy->xwky", forward_table, grid_field, precision=lax.Precision.HIGHEST
    )
    cosine_y, sine_y = wave_tables(NY, NY, NY)
    pencils = transform_rows(
        lax.all_to_all(spectra_z, "cell", split_axis=2, concat_axis=3, tiled=True),
        cosine_y,
        sine_y,
        1.0,
    )
    columns = lax.all_to_all(pencils, "slab", split_axis=3, concat_axis=0, tiled=True)
    col_width = columns.shape[2] * columns.shape[3]
    flat_rows = columns.reshape(NX, 2 * col_width)
    first_row = lax.axis_index("cell") * depth_count
    kernel_ids = lax.dynamic_slice_in_dim(freq_ids, first_row, depth_count, 0)
    kernel = jnp.take(spectrum, kernel_ids, axis=1).reshape(NX, col_width) * (1.0 / (NX * NY * NZ))
    kernel_both = jnp.concatenate([kernel, kernel], axis=1)
    slab_count = lax.axis_size("slab")
    local_rows = NX // slab_count
    cosine_s, sine_s = wave_tables(slab_count, slab_count, slab_count)
    cosine_r, sine_r = wave_tables(local_rows, local_rows, local_rows)
    twist_cos, twist_sin = wave_tables(slab_count, local_rows, NX)
    twist_cos = twist_cos[:, :, None]
    twist_sin = twist_sin[:, :, None]
    section_one = transform_axis(
        "ks,src->krc",
        cosine_s,
        sine_s,
        flat_rows.reshape(slab_count, local_rows, 2 * col_width),
        1.0,
    )
    section_one = twiddle(section_one, twist_cos, twist_sin, 1.0)
    section_two = transform_axis("jr,krc->jkc", cosine_r, sine_r, section_one, 1.0)
    weighted = section_two.reshape(NX, 2 * col_width) * kernel_both
    section_one = transform_axis(
        "rj,jkc->krc",
        cosine_r,
        sine_r,
        weighted.reshape(local_rows, slab_count, 2 * col_width),
        -1.0,
    )
    section_one = twiddle(section_one, twist_cos, twist_sin, -1.0)
    section_two = transform_axis("sk,krc->src", cosine_s, sine_s, section_one, -1.0)
    returned_x = section_two.reshape(NX, 2 * col_width)
    returned = lax.all_to_all(
        returned_x.reshape(columns.shape), "slab", split_axis=0, concat_axis=3, tiled=True
    )
    inverse_rows = transform_rows(returned, cosine_y, sine_y, -1.0)
    grid_potential = jnp.einsum(
        "wkz,xwky->xzy",
        backward_table,
        lax.all_to_all(inverse_rows, "cell", split_axis=3, concat_axis=2, tiled=True),
        precision=lax.Precision.HIGHEST,
    )
    tile_potential = (
        grid_potential.reshape(cell_planes, TX, NZC, TZ, rows_cell, TY)
        .transpose(1, 5, 3, 0, 4, 2)
        .reshape(TX * TY * TZ, cell_planes, cell_cols)
    )
    far_field = jnp.einsum(
        "ptxc,txc->pxc", projection, tile_potential, precision=lax.Precision.HIGHEST
    )
    block = masked.reshape(panels, cell_planes, rows_cell, NZC)
    extended = padded(block, (("slab", 1), ("cell", 2)), 1)
    flat_ext = extended.reshape(panels, -1)
    step_x = neighbours // 9 - 1
    step_y = neighbours // 3 % 3 - 1
    step_z = neighbours % 3 - 1
    plane_ids = lax.broadcasted_iota(jnp.int32, neighbours.shape, 1)
    col_ids = lax.broadcasted_iota(jnp.int32, neighbours.shape, 2)
    row_ids = col_ids // NZC
    depth_ids = col_ids % NZC
    near_ids = ((plane_ids + step_x + 1) * (rows_cell + 2) + row_ids + step_y + 1) * NZC + (
        depth_ids + step_z
    ) % NZC
    near_count = neighbours.shape[0]
    picked = jnp.take(flat_ext, near_ids.reshape(-1), axis=1).reshape(
        panels, near_count, cell_planes, cell_cols
    )
    near_field = jnp.einsum("kpqxc,qkxc->pxc", near_blocks, picked, precision=lax.Precision.HIGHEST)
    return (far_field + near_field) * panel_mask


def solution(mesh):
    in_specs = (
        P(None, "slab", "cell"),
        P("slab", "cell"),
        P(None, None, "slab", "cell"),
        P(None, None, None, "slab", "cell"),
        P(None, "slab", "cell"),
        P(None, None, "slab"),
    )
    out_specs = P(None, "slab", "cell")
    return jax.shard_map(
        per_device, mesh=mesh, in_specs=in_specs, out_specs=out_specs, check_vma=False
    )
```

profile of v0, /device:TPU:32, one launch (start us, length us, event | category | flops | bytes accessed | tf_op | source)
XLA Modules:
  0.0 227.6 jit_solution(5112245860628216884)
XLA Ops:
  0.2 0.8 fusion.138
  0.9 1.4 fusion.4
  2.3 0.4 reshape.361
  2.7 4.9 %copy.61 = f32[1,4,16,4,32,4]{5,4,3,2,1,0:T(8,128)} copy(f32[1,4,16,4,32,4]{2,4,3,5,1,0:T(8,128)S(1)} %bitcast.149) | data formatting | bytes 262144 | tf_op jit(solution)/shard_map/transpose | solution.py:100
  7.6 4.9 %reshape.389 = f32[4,64,128,1]{2,1,0,3:T(8,128)S(1)} reshape(f32[1,4,16,4,32,4]{5,4,3,2,1,0:T(8,128)} %copy.61) | data formatting | bytes 262144 | tf_op jit(solution)/shard_map/reshape | solution.py:101
  12.5 0.4 convolution_bitcast_fusion
  12.8 0.9 copy.62
  13.8 8.8 %all-to-all-start = ((f32[4,2,64,128]{3,1,0,2:T(2,128)}), f32[4,2,64,128]{3,1,0,2:T(2,128)S(1)}, u32[]{:S(2)}, u32[]{:S(2)}) async-start(f32[4,2,64,128]{3,1,0,2:T(2,128)} %copy.62), calls=%async_computation | async-start | bytes 524288 | tf_op jit(solution)/shard_map/all_to_all | solution.py:111
  22.7 11.2 %collective-permute-start.1 = (f32[8,1,32,16]{3,2,0,1:T(8,128)S(1)}, f32[8,1,32,16]{3,2,0,1:T(8,128)}, u32[]{:S(2)}, u32[]{:S(2)}) collective-permute-start(f32[8,1,32,16]{3,2,0,1:T(8,128)S(1)} %reshape.366), channel_id=1, source_target_pairs={{4,0},{8,4},{12,8},{16,12},{20,16},{24,20},{28,24},{32,28},{36,32}... | collective-permute-start | bytes 49160 | tf_op jit(solution)/shard_map/ppermute | solution.py:25
  33.9 2.4 %collective-permute-start = (f32[8,1,32,16]{3,2,0,1:T(8,128)S(1)}, f32[8,1,32,16]{3,2,0,1:T(8,128)}, u32[]{:S(2)}, u32[]{:S(2)}) collective-permute-start(f32[8,1,32,16]{3,2,0,1:T(8,128)S(1)} %reshape.366), channel_id=1, source_target_pairs={{0,4},{4,8},{8,12},{12,16},{16,20},{20,24},{24,28},{28,32},{32,36}... | collective-permute-start | bytes 49160 | tf_op jit(solution)/shard_map/ppermute | solution.py:24
  36.4 0.2 copy.127
  36.7 4.9 %fusion.11 = f32[4,2,16,512]{3,2,1,0:T(8,128)S(1)} fusion(f32[4,2,16,512]{3,2,1,0:T(8,128)S(1)} %dot_general.60), kind=kOutput, calls=%fused_computation.21 | convolution fusion | flops 406323200 | bytes 524288 | tf_op jit(solution)/shard_map/dot_general | solution.py:82
  41.6 4.9 %fusion.7 = f32[4,2,16,512]{3,2,1,0:T(8,128)S(1)} fusion(f32[4,2,16,512]{3,2,1,0:T(8,128)S(1)} %dot_general.60), kind=kOutput, calls=%fused_computation.17 | convolution fusion | flops 406323200 | bytes 524288 | tf_op jit(solution)/shard_map/dot_general | solution.py:79
  46.6 1.5 copy.64
  48.1 3.6 %reshape.411 = f32[128,1,512]{2,1,0:T(1,128)} reshape(f32[512,4,2,16]{3,2,1,0:T(2,128)S(1)} %bitcast.142) | data formatting | bytes 524288
  51.7 16.5 %all-to-all-start.1 = ((f32[128,1,512]{2,1,0:T(1,128)}), f32[128,1,512]{2,1,0:T(1,128)S(1)}, u32[]{:S(2)}, u32[]{:S(2)}) async-start(f32[128,1,512]{2,1,0:T(1,128)} %reshape.411), calls=%async_computation.1 | async-start | bytes 524288 | tf_op jit(solution)/shard_map/all_to_all | solution.py:116
  68.4 0.6 gather_fusion
  69.1 0.2 copy.69
  69.4 0.3 fusion.53
  69.8 24.2 %all-to-all-done.1 = f32[128,1,512]{2,1,0:T(1,128)S(1)} async-done(((f32[128,1,512]{2,1,0:T(1,128)}), f32[128,1,512]{2,1,0:T(1,128)S(1)}, u32[]{:S(2)}, u32[]{:S(2)}) %all-to-all-start.1) | async-done | bytes 262176 | tf_op jit(solution)/shard_map/all_to_all | solution.py:116
  94.0 0.5 broadcast.502
  94.5 1.3 reduce.8
  95.8 2.8 %reshape.412 = f32[512,4,2,16]{3,2,1,0:T(2,128)S(1)} reshape(f32[128,512]{1,0:T(8,128)S(1)} %reduce.8) | data formatting | bytes 524288
  98.6 1.7 copy.65
  100.3 1.8 copy.66
  102.1 0.6 fusion.49
  102.8 0.6 fusion.45
  103.7 0.6 fusion.72
  104.3 0.6 fusion.76
  104.9 0.3 slice_add_fusion
  105.2 0.8 fusion.70
  106.1 0.8 fusion.74
  107.3 0.6 fusion.47
  107.9 0.6 fusion.43
  108.8 10.2 %reshape_reshape.7 = f32[512,2,16,4]{3,2,1,0:T(8,128)} reshape(f32[128,4,128]{2,1,0:T(4,128)S(1)} %copy.72) | data formatting | bytes 524288 | tf_op jit(solution)/shard_map/reshape;reshape | solution.py:151
  119.0 8.3 %copy.73 = f32[512,2,16,4]{2,3,1,0:T(4,128)S(1)} copy(f32[512,2,16,4]{3,2,1,0:T(8,128)} %reshape_reshape.7) | data formatting | bytes 524288 | tf_op jit(solution)/shard_map/reshape;reshape | solution.py:151
  127.3 2.3 %reshape.413 = f32[128,1,512]{2,1,0:T(1,128)} reshape(f32[512,2,4,16]{3,2,1,0:T(4,128)S(1)} %bitcast.141) | data formatting | bytes 524288
  129.6 6.2 %all-to-all-start.2 = ((f32[128,1,512]{2,1,0:T(1,128)}), f32[128,1,512]{2,1,0:T(1,128)S(1)}, u32[]{:S(2)}, u32[]{:S(2)}) async-start(f32[128,1,512]{2,1,0:T(1,128)} %reshape.413), calls=%async_computation.2 | async-start | bytes 524288 | tf_op jit(solution)/shard_map/all_to_all | solution.py:150
  135.8 0.9 constant_dynamic-update-slice_fusion.2
  136.7 0.9 constant_dynamic-update-slice_fusion
  137.7 3.7 %collective-permute-start.2 = (f32[8,3,1,16]{3,2,0,1:T(1,128)S(1)}, f32[8,3,1,16]{3,2,0,1:T(1,128)S(1)}, u32[]{:S(2)}, u32[]{:S(2)}) collective-permute-start(f32[8,3,1,16]{3,2,0,1:T(1,128)S(1)} %get-tuple-element.21), channel_id=1, source_target_pairs={{0,1},{1,2},{2,3},{3,0},{4,5},{5,6},{6,7},{7,4},{8,9},{9,10},{10,1... | collective-permute-start | bytes 4616 | tf_op jit(solution)/shard_map/ppermute | solution.py:24
  141.3 2.2 collective-permute-start.3
  143.5 18.8 %all-to-all-done.2 = f32[128,1,512]{2,1,0:T(1,128)S(1)} async-done(((f32[128,1,512]{2,1,0:T(1,128)}), f32[128,1,512]{2,1,0:T(1,128)S(1)}, u32[]{:S(2)}, u32[]{:S(2)}) %all-to-all-start.2) | async-done | bytes 262176 | tf_op jit(solution)/shard_map/all_to_all | solution.py:150
  162.3 1.3 reduce.9
  163.5 1.5 reshape.414
  165.1 0.4 copy.74
  165.5 1.4 copy.75
  166.8 10.0 %fusion.9 = f32[4,2,16,512]{3,2,1,0:T(8,128)S(1)} fusion(f32[4,2,16,512]{2,3,1,0:T(8,128)S(1)} %bitcast.155), kind=kOutput, calls=%fused_computation.19 | convolution fusion | flops 406323200 | bytes 524288 | tf_op jit(solution)/shard_map/dot_general | solution.py:82
  176.8 9.6 %fusion.5 = f32[4,2,16,512]{3,2,1,0:T(8,128)S(1)} fusion(f32[4,2,16,512]{2,3,1,0:T(8,128)S(1)} %bitcast.156), kind=kOutput, calls=%fused_computation.15 | convolution fusion | flops 406323200 | bytes 524288 | tf_op jit(solution)/shard_map/dot_general | solution.py:79
  186.5 1.5 copy.78
  187.9 3.6 %reshape.415 = f32[4,1,16384]{2,1,0:T(1,128)} reshape(f32[512,4,2,16]{3,2,1,0:T(2,128)S(1)} %bitcast.143) | data formatting | bytes 524288
  191.5 3.6 %all-to-all-start.3 = ((f32[4,1,16384]{2,1,0:T(1,128)}), f32[4,1,16384]{2,1,0:T(1,128)S(1)}, u32[]{:S(2)}, u32[]{:S(2)}) async-start(f32[4,1,16384]{2,1,0:T(1,128)} %reshape.415), calls=%async_computation.3 | async-start | bytes 524288 | tf_op jit(solution)/shard_map/all_to_all | solution.py:157
  195.2 0.3 copy.82
  195.6 10.9 %gather_fusion.1 = f32[3072,8]{1,0:T(8,128)} fusion(f32[8,1632]{0,1:T(8,128)S(1)} %bitcast.150, s32[3072]{0:T(1024)S(1)} %broadcast_clamp_fusion), kind=kCustom, calls=%fused_computation.1 | custom fusion | bytes 208896 | tf_op jit(solution)/shard_map/jit(_take)/gather | solution.py:182
  206.5 1.8 select_bitcast_fusion
  208.3 0.4 copy.116
  208.8 1.4 reduce.10
  210.2 2.8 %reshape.416 = f32[512,4,2,16]{3,2,1,0:T(2,128)S(1)} reshape(f32[4,16384]{1,0:T(4,128)S(1)} %reduce.10) | data formatting | bytes 524288
  213.0 1.4 copy.79
  214.4 0.3 convolution_bitcast_fusion.1
  214.8 5.7 %reshape.363 = f32[1,4,16,4,32,4]{5,4,3,2,1,0:T(8,128)} reshape(f32[4,64,128]{2,1,0:T(8,128)S(1)} %convolution_bitcast_fusion.1) | data formatting | bytes 262144 | tf_op jit(solution)/shard_map/reshape | solution.py:161
  220.4 5.5 %copy.81 = f32[4,4,4,1,32,16]{5,4,2,1,0,3:T(8,128)S(1)} copy(f32[4,4,4,1,32,16]{1,4,2,5,0,3:T(8,128)} %bitcast.140) | data formatting | bytes 262144 | tf_op jit(solution)/shard_map/transpose | solution.py:162
  226.0 0.6 reshape.364
  226.8 0.6 compare_select_fusion.4
  (55 shorter events, 2.2 us)
Async XLA Ops:
  0.0 68.4 %copy-start = (f32[512,64,4]{0,2,1:T(4,128)S(1)}, f32[512,64,4]{0,2,1:T(4,128)}, u32[]{:S(2)}) copy-start(f32[512,64,4]{0,2,1:T(4,128)} %param.11) | copy-start | bytes 1572868
  13.8 22.7 %all-to-all-start = ((f32[4,2,64,128]{3,1,0,2:T(2,128)}), f32[4,2,64,128]{3,1,0,2:T(2,128)S(1)}, u32[]{:S(2)}, u32[]{:S(2)}) async-start(f32[4,2,64,128]{3,1,0,2:T(2,128)} %copy.62), calls=%async_computation | async-start | bytes 524288 | tf_op jit(solution)/shard_map/all_to_all | solution.py:111
  22.7 114.0 %collective-permute-start.1 = (f32[8,1,32,16]{3,2,0,1:T(8,128)S(1)}, f32[8,1,32,16]{3,2,0,1:T(8,128)}, u32[]{:S(2)}, u32[]{:S(2)}) collective-permute-start(f32[8,1,32,16]{3,2,0,1:T(8,128)S(1)} %reshape.366), channel_id=1, source_target_pairs={{4,0},{8,4},{12,8},{16,12},{20,16},{24,20},{28,24},{32,28},{36,32}... | collective-permute-start | bytes 49160 | tf_op jit(solution)/shard_map/ppermute | solution.py:25
  33.9 101.9 %collective-permute-start = (f32[8,1,32,16]{3,2,0,1:T(8,128)S(1)}, f32[8,1,32,16]{3,2,0,1:T(8,128)}, u32[]{:S(2)}, u32[]{:S(2)}) collective-permute-start(f32[8,1,32,16]{3,2,0,1:T(8,128)S(1)} %reshape.366), channel_id=1, source_target_pairs={{0,4},{4,8},{8,12},{12,16},{16,20},{20,24},{24,28},{28,32},{32,36}... | collective-permute-start | bytes 49160 | tf_op jit(solution)/shard_map/ppermute | solution.py:24
  51.7 42.3 %all-to-all-start.1 = ((f32[128,1,512]{2,1,0:T(1,128)}), f32[128,1,512]{2,1,0:T(1,128)S(1)}, u32[]{:S(2)}, u32[]{:S(2)}) async-start(f32[128,1,512]{2,1,0:T(1,128)} %reshape.411), calls=%async_computation.1 | async-start | bytes 524288 | tf_op jit(solution)/shard_map/all_to_all | solution.py:116
  68.4 1.0 copy-start.3
  129.6 32.7 %all-to-all-start.2 = ((f32[128,1,512]{2,1,0:T(1,128)}), f32[128,1,512]{2,1,0:T(1,128)S(1)}, u32[]{:S(2)}, u32[]{:S(2)}) async-start(f32[128,1,512]{2,1,0:T(1,128)} %reshape.413), calls=%async_computation.2 | async-start | bytes 524288 | tf_op jit(solution)/shard_map/all_to_all | solution.py:150
  137.7 57.5 %collective-permute-start.2 = (f32[8,3,1,16]{3,2,0,1:T(1,128)S(1)}, f32[8,3,1,16]{3,2,0,1:T(1,128)S(1)}, u32[]{:S(2)}, u32[]{:S(2)}) collective-permute-start(f32[8,3,1,16]{3,2,0,1:T(1,128)S(1)} %get-tuple-element.21), channel_id=1, source_target_pairs={{0,1},{1,2},{2,3},{3,0},{4,5},{5,6},{6,7},{7,4},{8,9},{9,10},{10,1... | collective-permute-start | bytes 4616 | tf_op jit(solution)/shard_map/ppermute | solution.py:24
  141.3 53.8 %collective-permute-start.3 = (f32[8,3,1,16]{3,2,0,1:T(1,128)S(1)}, f32[8,3,1,16]{3,2,0,1:T(1,128)S(1)}, u32[]{:S(2)}, u32[]{:S(2)}) collective-permute-start(f32[8,3,1,16]{3,2,0,1:T(1,128)S(1)} %get-tuple-element.22), channel_id=1, source_target_pairs={{1,0},{2,1},{3,2},{0,3},{5,4},{6,5},{7,6},{4,7},{9,8},{10,9},{11,1... | collective-permute-start | bytes 4616 | tf_op jit(solution)/shard_map/ppermute | solution.py:25
  191.5 17.3 %all-to-all-start.3 = ((f32[4,1,16384]{2,1,0:T(1,128)}), f32[4,1,16384]{2,1,0:T(1,128)S(1)}, u32[]{:S(2)}, u32[]{:S(2)}) async-start(f32[4,1,16384]{2,1,0:T(1,128)} %reshape.415), calls=%async_computation.3 | async-start | bytes 524288 | tf_op jit(solution)/shard_map/all_to_all | solution.py:157
  206.5 2.2 copy-start.2
  220.4 6.1 %copy-start.1 = (f32[8,64,1,512]{3,2,1,0:T(1,128)S(1)}, f32[8,64,1,512]{3,2,1,0:T(1,128)}, u32[]{:S(2)}) copy-start(f32[8,64,1,512]{3,2,1,0:T(1,128)} %param.8) | copy-start | bytes 3145732
  225.9 0.8 copy-start.4
where the time goes:
time: 232 us; the launch traced here: 228 us
  local copies, waits for them, and re-layouts  83.6 us (36%)
  starting transfers between devices  54.5 us (23%)
  waiting for transfers between devices  43 us (19%)
  matrix products  35.4 us (15%)
  other arithmetic  10.2 us (4%)
    all_to_all x1, waiting for transfers between devices, per_device(): lax.all_to_all(pencils, 'slab', split_axis=3, concat_axis=0, tiled=True)  24.2 us
    all_to_all x1, waiting for transfers between devices, per_device(): lax.all_to_all(returned_x.reshape(columns.shape), 'slab', split_axis=0, c...  18.8 us
    another operation x2, local copies, waits for them, and re-layouts, per_device(): returned_x.reshape(columns.shape)  18.5 us
    unnamed x20, local copies, waits for them, and re-layouts  18 us
    all_to_all x1, starting transfers between devices, per_device(): lax.all_to_all(pencils, 'slab', split_axis=3, concat_axis=0, tiled=True)  16.5 us
    dot_general x2, matrix products, transform_rows(): jnp.dot(flat_rows, sine_tab, precision=lax.Precision.HIGHEST)  14.9 us
    dot_general x2, matrix products, transform_rows(): jnp.dot(flat_rows, cosine, precision=lax.Precision.HIGHEST)  14.4 us
    ppermute x2, starting transfers between devices, padded(): after = lax.ppermute(first, axis, down)  13.4 us
  transfers between devices with their start and end apart: 8, of which 2 were waited for; matrix products, arithmetic and copies ran while one was open for 43% of the time, Pallas kernels for 0%

commit v1 on v0

v1 whole, which is shorter than its diff:
```python
import functools

import jax
import jax.numpy as jnp
import numpy as np
from jax import lax
from jax.experimental import pallas as pl
from jax.experimental.pallas import tpu as pltpu
from jax.sharding import PartitionSpec as P

F32 = jnp.float32
BF16 = jnp.bfloat16
NZ_RING = 16
NU = 32
SCALE = 1.0 / 16777216.0
POS_OF_K2 = (0, 2, 1, 3)


def split_np(table):
    hi = table.astype(np.float32).astype(jnp.bfloat16)
    lo = (table - hi.astype(np.float64)).astype(jnp.bfloat16)
    return hi, lo


def cis(num, den):
    ang = 2.0 * np.pi * (num % den) / den
    return np.cos(ang), np.sin(ang)


def slot_freq(z, j):
    return z + 16 * j


def z_table():
    tab = np.zeros((16, 2, 2, 4, 8, 16))
    zc = np.arange(16)
    for z in range(16):
        for j in range(2):
            for tz in range(4):
                gz = zc * 4 + tz
                if z == 0 and j == 0:
                    re, im = np.ones(16), 1.0 - 2.0 * (gz % 2)
                else:
                    c, s = cis(slot_freq(z, j) * gz, 64)
                    re, im = c, -s
                tab[z, 0, j, tz] = re
                tab[z, 1, j, tz] = im
    return tab.reshape(64, 512)


def z_table_wide():
    tab = z_table().reshape(16, 2, 1, 2, 512)
    return np.broadcast_to(tab, (16, 2, 4, 2, 512)).reshape(256, 512)


def y_table():
    r8, ty, l = np.meshgrid(np.arange(8), np.arange(4), np.arange(4), indexing="ij")
    low = (l * 32 + r8 * 4 + ty).reshape(-1)
    k0, u, zq = np.meshgrid(np.arange(4), np.arange(32), np.arange(4), indexing="ij")
    ky = zq * 128 + u * 4 + k0
    c, s = cis(ky[..., None] * low, 512)
    tab = np.zeros((4, 32, 2, 4, 2, 128))
    tab[:, :, 0, :, 0] = c
    tab[:, :, 0, :, 1] = s
    tab[:, :, 1, :, 0] = -s
    tab[:, :, 1, :, 1] = c
    return tab.reshape(4, 256, 256)


def x_table():
    c, s = cis(np.arange(32)[:, None] * np.arange(32)[None, :], 32)
    tab = np.zeros((32, 2, 4, 32, 2, 4))
    for q in range(4):
        tab[:, 0, q, :, 0, q] = c
        tab[:, 0, q, :, 1, q] = s
        tab[:, 1, q, :, 0, q] = -s
        tab[:, 1, q, :, 1, q] = c
    return tab.reshape(256, 256)


def lane_parts():
    lane = np.arange(128)
    return lane // 32, (lane // 8) % 4, (lane // 2) % 4, lane % 2


def twist_table(u_or_k1, second):
    k0, kx0, tx, _ = lane_parts()
    row = np.arange(32)[:, None]
    num = tx[None] * (kx0[None] + 4 * row) if second else 4 * row * kx0[None]
    c, s = cis(num, 512)
    cc = np.zeros((32, 2, 4, 128))
    ss = np.zeros((32, 2, 4, 128))
    cc[:] = c[:, None, None, :]
    ss[:, 0] = s[:, None, :]
    ss[:, 1] = -s[:, None, :]
    return cc.reshape(256, 128).astype(np.float32), ss.reshape(256, 128).astype(np.float32)


def pick_table():
    tab = np.zeros((32, 2, 4, 4, 128))
    for k1 in range(32):
        for q in range(4):
            tab[k1, :, q, q, 4 * k1 : 4 * k1 + 4] = 1.0
    return tab.reshape(256, 512)


@functools.cache
def tables():
    out = []
    zt = z_table()
    out += list(split_np(zt))
    out += list(split_np(y_table()))
    g = x_table()
    out += list(split_np(g))
    out += list(split_np(g.T))
    out += list(twist_table(None, False))
    out += list(twist_table(None, True))
    out.append(pick_table().astype(jnp.bfloat16))
    out += list(split_np(z_table_wide()))
    return tuple(np.asarray(t) for t in out)


def roll(x, shift, axis):
    if axis == 1 and x.shape[1] > 128:
        return jnp.concatenate([roll(x[:, i : i + 128], shift, 1) for i in range(0, x.shape[1], 128)], axis=1)
    return pltpu.roll(x, shift % x.shape[axis], axis)


def sub4(x):
    return roll(x, 4, 0)


def iota(shape, dim):
    return lax.broadcasted_iota(jnp.int32, shape, dim)


def split(x):
    hi = x.astype(BF16)
    return hi, (x - hi.astype(F32)).astype(BF16)


NN = (((1,), (0,)), ((), ()))
NT = (((1,), (1,)), ((), ()))


def dot(a, b, dims):
    return lax.dot_general(a, b, dims, preferred_element_type=F32)


def dot3(ah, al, bh, bl, dims):
    return dot(ah, bh, dims) + (dot(al, bh, dims) + dot(ah, bl, dims))


def four_point(parts, sign):
    (ar, ai), (br, bi), (cr, ci), (dr, di) = parts
    pr, pi, mr, mi = ar + cr, ai + ci, ar - cr, ai - ci
    qr, qi, nr, ni = br + dr, bi + di, br - dr, bi - di
    if sign < 0:
        return [(pr + qr, pi + qi), (mr + ni, mi - nr), (pr - qr, pi - qi), (mr - ni, mi + nr)]
    return [(pr + qr, pi + qi), (mr - ni, mi + nr), (pr - qr, pi - qi), (mr + ni, mi - nr)]


def lane_partner(x, stride, bit):
    return jnp.where(bit == 0, roll(x, -stride, 1), roll(x, stride, 1))


def swap_signed(x, ri, sign):
    r = sub4(x)
    return jnp.where(ri == 0, -r, r) if sign > 0 else jnp.where(ri == 0, r, -r)


def lane_dft4(x, sign):
    lane = iota(x.shape, 1)
    ri = (iota(x.shape, 0) >> 2) & 1
    b1, b0 = (lane >> 2) & 1, (lane >> 1) & 1
    if sign < 0:
        a = lane_partner(x, 4, b1)
        x = jnp.where(b1 == 0, x + a, a - x)
        x = jnp.where((b1 == 1) & (b0 == 1), swap_signed(x, ri, -1), x)
        c = lane_partner(x, 2, b0)
        return jnp.where(b0 == 0, x + c, c - x)
    c = lane_partner(x, 2, b0)
    x = jnp.where(b0 == 0, x + c, c - x)
    x = jnp.where((b1 == 1) & (b0 == 1), swap_signed(x, ri, 1), x)
    a = lane_partner(x, 4, b1)
    return jnp.where(b1 == 0, x + a, a - x)


def masked_charges(ch, cnt):
    row = iota((8, 128), 0)
    return [jnp.where(2 * i + (row >> 2) < cnt, ch(i), 0.0) for i in range(4)]


def both_halves(mv):
    row = iota((8, 128), 0)
    out = []
    for v in mv:
        r = sub4(v)
        out += [jnp.where(row < 4, v, r), jnp.where(row < 4, r, v)]
    return out


def tiles_of(proj, m):
    out = []
    for v in range(32):
        acc = proj(0, v) * m[0]
        for p in range(1, 8):
            acc = acc + proj(p, v) * m[p]
        out.append(acc)
    return out


def regroup(tile):
    low = iota((8, 128), 0) < 4
    base = [[[None] * 4 for _ in range(2)] for _ in range(4)]
    for tx in range(4):
        for a in range(2):
            for h in range(2):
                v0, v1 = tile[tx * 8 + 4 * a + h], tile[tx * 8 + 4 * a + 2 + h]
                base[tx][a][2 * h] = jnp.where(low, v0, sub4(v1))
                base[tx][a][2 * h + 1] = jnp.where(low, sub4(v0), v1)
    return base


def ungroup(e):
    low = iota((8, 128), 0) < 4
    out = [None] * 32
    for tx in range(4):
        for a in range(2):
            for h in range(2):
                p, q = e[tx][a][2 * h], e[tx][a][2 * h + 1]
                out[tx * 8 + 4 * a + h] = jnp.where(low, p, sub4(q))
                out[tx * 8 + 4 * a + 2 + h] = jnp.where(low, sub4(p), q)
    return out


def y_fixup(whole, part, k0, off):
    lane, row = iota(whole.shape, 1), iota(whole.shape, 0)
    zq, ri, u = lane & 3, (lane >> 2) & 1, lane >> 3
    rest = whole - part
    swapped = jnp.where(ri == 0, roll(rest, -4, 1), -roll(rest, 4, 1))
    alone = (u == 0) & ((zq & 1) == 0) if k0 == 0 else (lane < 0)
    special = ((row & 1) + off == 0) & jnp.logical_not(alone)
    return jnp.where(special, jnp.where(zq < 2, part, swapped), whole)


def y_forward(whole, part, fh, fl, off):
    rows = []
    for k0 in range(4):
        x = jnp.concatenate(
            [
                jnp.concatenate([jnp.concatenate(y[k0], axis=0) for y in pair], axis=1)
                for pair in (whole, part)
            ],
            axis=0,
        )
        xh, xl = split(x)
        o = dot3(xh, xl, fh(k0), fl(k0), NT)
        rows.append(y_fixup(o[:32], o[32:], k0, off))
    return jnp.concatenate(rows, axis=0).T


def y_backward(v, fh, fl, off):
    vt = v.T
    first, second = ([], []), ([], [])
    for k0 in range(4):
        a = vt[k0 * 32 : k0 * 32 + 32]
        lane, row = iota(a.shape, 1), iota(a.shape, 0)
        zq, ri, u = lane & 3, (lane >> 2) & 1, lane >> 3
        special = (row & 1) + off == 0
        alone = (u == 0) & ((zq & 1) == 0) if k0 == 0 else (lane < 0)
        va = jnp.where(special & (zq >= 2) & jnp.logical_not(alone), 0.0, a)
        vb = jnp.where(zq >= 2, a, 0.0)
        if k0 == 0:
            vb = jnp.where(alone, jnp.where(ri == 0, roll(a, -4, 1), -roll(a, 4, 1)), vb)
        xh, xl = split(jnp.concatenate([va, vb], axis=0))
        o = dot3(xh, xl, fh(k0), fl(k0), NN)
        for half, pair in enumerate((first, second)):
            for ri_part in range(2):
                pair[ri_part].append(
                    [
                        o[32 * half + 8 * q : 32 * half + 8 * q + 8, 128 * ri_part : 128 * ri_part + 128]
                        for q in range(4)
                    ]
                )
    return first, second


def low_forward(r1):
    inner = [
        four_point([(r1(zh * 4 + zl, 0), r1(zh * 4 + zl, 1)) for zl in range(4)], -1)
        for zh in range(4)
    ]
    yr, yi = [], []
    for k0 in range(4):
        o = four_point([inner[zh][k0] for zh in range(4)], -1)
        yr.append([p[0] for p in o])
        yi.append([p[1] for p in o])
    return yr, yi


def low_backward(y):
    inner = [four_point(list(zip(y[0][k0], y[1][k0])), 1) for k0 in range(4)]
    return [four_point([inner[k0][zh] for k0 in range(4)], 1) for zh in range(4)]


def merge_planes(first, second, off):
    special = (iota((8, 128), 0) & 1) + off == 0
    a, b = low_backward(first), low_backward(second)
    return [
        (a[z // 4][z % 4][0], jnp.where(special, b[z // 4][z % 4][0], a[z // 4][z % 4][1]))
        for z in range(16)
    ]


def twist(x, c, s):
    return x * c + sub4(x) * s


def x_input(r2, tc, ts):
    lane, row = iota((8, 128), 1), iota((8, 128), 0)
    kx0 = (lane >> 3) & 3
    main, conj = [], []
    for u in range(32):
        v = r2(u)
        w = jnp.where(kx0 == 1, roll(v, -16, 1), jnp.where(kx0 == 3, roll(v, 16, 1), v))
        w = jnp.where(row < 4, w, -w)
        main.append(twist(v, tc(u), ts(u)))
        conj.append(twist(w, tc(u), ts(u)))
    return jnp.concatenate(
        [jnp.concatenate(main, axis=0), jnp.concatenate(conj, axis=0)], axis=1
    )


def x_middle(q, k1, tc, ts, c1, c2):
    a = lane_dft4(twist(q[:, :128], tc, ts), -1)
    b = lane_dft4(twist(q[:, 128:], tc, ts), -1)
    return twist(lane_dft4(a * c1 + b * c2, 1), tc, -ts)


def coefficients(sm, sa, off, off_u):
    lane, row = iota((8, 128), 1), iota((8, 128), 0)
    zq = row & 3
    special = (lane >> 5) + (lane & 1) + (zq & 1) + off + off_u == 0
    c1 = jnp.where(special, 0.5 * SCALE * (sm + sa), 2.0 * SCALE * sm)
    half = 0.5 * SCALE * (sm - sa)
    c2 = jnp.where(special, jnp.where(zq < 2, half, -half), 0.0)
    return c1, c2


def spread_spectrum(rows, pick):
    lane = iota((8, 128), 1)
    keep = [(lane & 3) == kx0 for kx0 in range(4)]
    cols = []
    for zq in range(4):
        parts = []
        for alt in range(2):
            b = rows(zq, alt)
            for k0 in range(4):
                for kx0 in range(4):
                    parts.append(jnp.where(keep[kx0], b[8 * k0 : 8 * k0 + 8], 0.0))
        cols.append(jnp.concatenate(parts, axis=0))
    m = jnp.concatenate(cols, axis=1)
    h, l = split(m)
    return dot(pick, h, NT) + dot(pick, l, NT)


def z_backward_fold(o):
    lane = iota((8, 128), 1)
    e = [[[None] * 4 for _ in range(2)] for _ in range(4)]
    for tx in range(4):
        for a in range(2):
            for tz in range(4):
                acc = o(tx, 0, a, tz)
                for r8 in range(1, 8):
                    acc = jnp.where((lane >> 4) == r8, o(tx, r8, a, tz), acc)
                e[tx][a][tz] = acc
    return e


def far_of(proj, pot):
    out = []
    for p in range(8):
        acc = proj(p, 0) * pot[0]
        for v in range(1, 32):
            acc = acc + proj(p, v) * pot[v]
        out.append(acc)
    return out


def near_of(plane, above, below, codes, near):
    lane, row = iota((8, 128), 1), iota((8, 128), 0)
    l, zc = row & 3, lane & 15
    code = [codes(k) for k in range(6)]
    picked = [[jnp.zeros((8, 128), F32)] * 4 for _ in range(6)]
    for d in range(3):
        for i in range(4):
            v = plane(d, i)
            up = roll(v, -16, 1)
            nxt = jnp.where(l == 3, roll(below(d, i), -16, 1), roll(up, -1, 0))
            after = jnp.where(lane >= 112, nxt, up)
            dn = roll(v, 16, 1)
            prv = jnp.where(l == 0, roll(above(d, i), 16, 1), roll(dn, 1, 0))
            before = jnp.where(lane < 16, prv, dn)
            for e, w in enumerate((before, v, after)):
                plus = jnp.where(zc == 15, roll(w, 15, 1), roll(w, -1, 1))
                minus = jnp.where(zc == 0, roll(w, -15, 1), roll(w, 1, 1))
                for f, x in enumerate((minus, w, plus)):
                    for k in range(6):
                        if k == 0 and (d, e, f) != (1, 1, 1):
                            continue
                        if k > 0 and (d, e, f) == (1, 1, 1):
                            continue
                        picked[k][i] = (
                            x if k == 0 else jnp.where(code[k] == 9 * d + 3 * e + f, x, picked[k][i])
                        )
    out = []
    for p in range(8):
        acc = None
        for k in range(6):
            for i in range(4):
                t = near(k, p, i) * picked[k][i]
                acc = t if acc is None else acc + t
        out.append(acc)
    return out


def z_order():
    out = []
    for step in range(8, 0, -1):
        out += [step] if step == 8 else [step, 16 - step]
    return out


def u_order():
    far = (0, 1, 2, 1)
    out = [(x, y, c) for x in range(4) for y in range(4) for c in range(2)]
    out.remove((0, 0, 0))
    return sorted(out, key=lambda t: (-far[t[0]] - far[t[1]], t))


def body(
    ch,
    cnt,
    proj,
    near,
    nbr,
    spec,
    *rest,
):
    tab_in, (out,), scr = rest[:15], rest[15:16], rest[16:]
    tab = scr[:15]
    (ch_s, cnt_s, proj_s, near_s, nbr_s) = scr[15:20]
    (sp, bm, nd, tp_h, tp_l) = scr[20:25]
    (s1, r1, s2, r2, s3, r3, s4, r4) = scr[25:33]
    (ms, bf, bl, hp, ha, hb, cc) = scr[33:40]
    (in_sem, tab_sem, loc_sem, snd, rcv) = scr[40:]
    (wzh, wzl, fh, fl, gh, gl, gth, gtl, t1c, t1s, t2c, t2s, pick, wxh, wxl) = tab

    slab, zl = lax.axis_index("slab"), lax.axis_index("cell")
    slabs = lax.axis_size("slab")
    zh, u = slab // NU, slab % NU
    z = zh * 4 + zl
    off = z
    off_u = u

    def z_peer(d):
        t = (z + d) % 16
        return t, ((t // 4) * NU + u, t % 4)

    def u_peer(d):
        t = ((u // 8 + d[0]) % 4) * 8 + ((u // 2 % 4 + d[1]) % 4) * 2 + (u + d[2]) % 2
        return t, (zh * NU + t, zl)

    def near_peer(e, f):
        return ((slab + slabs + e) % slabs, (zl + 4 + f) % 4)

    halo = [(e, f) for e in (-1, 0, 1) for f in (-1, 0, 1) if (e, f) != (0, 0)]

    first = [
        pltpu.make_async_copy(a, b, in_sem.at[i])
        for i, (a, b) in enumerate(
            ((ch, ch_s), (cnt, cnt_s), (proj, proj_s), (nbr, nbr_s), (near, near_s))
        )
    ]
    load = [pltpu.make_async_copy(a, b, tab_sem.at[i]) for i, (a, b) in enumerate(zip(tab_in, tab))]
    for c in first[:3] + load[:2]:
        c.start()

    barrier = pltpu.get_barrier_semaphore()
    peers = [z_peer(d)[1] for d in z_order()] + [u_peer(d)[1] for d in u_order()]
    peers += [near_peer(e, f) for e, f in halo]
    for p in peers:
        pl.semaphore_signal(barrier, inc=1, device_id=p, device_id_type=pl.DeviceIdType.MESH)
    for c in load[2:] + first[3:]:
        c.start()
    own = [
        pltpu.make_async_copy(spec.at[z + 16 * j], sp.at[zh, j], loc_sem.at[j]) for j in range(3)
    ]
    for c in own:
        c.start()

    def send(src, dst, i, dev):
        pltpu.make_async_remote_copy(
            src_ref=src,
            dst_ref=dst,
            send_sem=snd.at[i],
            recv_sem=rcv.at[i],
            device_id=dev,
            device_id_type=pl.DeviceIdType.MESH,
        ).start()

    def done(sem, i, ref):
        pltpu.make_async_copy(ref, ref, sem.at[i]).wait()

    first[0].wait()
    first[1].wait()
    half = cnt_s[...]
    cc[0:4, :] = half
    cc[4:8, :] = half
    mv = masked_charges(lambda i: ch_s[8 * i : 8 * i + 8, :], cc[...])
    for i in range(4):
        ms[8 * i : 8 * i + 8, :] = mv[i]
        for h in range(2):
            bf[2 * i + h : 2 * i + h + 1, :] = mv[i][4 * h : 4 * h + 1]
            bl[2 * i + h : 2 * i + h + 1, :] = mv[i][4 * h + 3 : 4 * h + 4]
    m = both_halves(mv)
    first[2].wait()

    def proj_at(p, v):
        r = (p * 32 + v) * 8
        return proj_s[r : r + 8, :]

    base = regroup(tiles_of(proj_at, m))
    lane16 = iota((16, 128), 1)
    keep = [jnp.where((lane16 >> 4) == r8, 1.0, 0.0).astype(BF16) for r8 in range(8)]
    for tx in range(4):
        for tz in range(4):
            h, l = split(jnp.concatenate([base[tx][0][tz], base[tx][1][tz]], axis=0))
            for r8 in range(8):
                r = tx * 128 + r8 * 16
                tp_h[r : r + 16, tz * 128 : tz * 128 + 128] = h * keep[r8]
                tp_l[r : r + 16, tz * 128 : tz * 128 + 128] = l * keep[r8]
    load[0].wait()
    load[1].wait()
    o = dot3(wzh[...], wzl[...], tp_h[...], tp_l[...], NT)
    for t in range(16):
        for ri in range(2):
            for tx in range(4):
                r = t * 4 + ri * 2
                s1[t, ri, 2 * tx : 2 * tx + 2, :] = o[r : r + 2, tx * 128 : tx * 128 + 128]
    pl.semaphore_wait(barrier, len(peers))
    for d in z_order():
        t, dev = z_peer(d)
        send(s1.at[t], r1.at[z], 0, dev)
    r1[pl.ds(z, 1)] = s1[pl.ds(z, 1)]

    for d in (2, 1, 3):
        th = (zh + d) % 4
        dev = (th * NU + u, zl)
        tz_id = th * 4 + zl
        for j in range(2):
            send(spec.at[tz_id + 16 * j], sp.at[zh, j], 4, dev)

        @pl.when(tz_id == 0)
        def _():
            send(spec.at[tz_id + 32], sp.at[zh, 2], 5, dev)

    for e, f in halo:
        dev = near_peer(e, f)
        if f == 0:
            send(ms, hp.at[(1 - e) // 2], 6 + (1 - e) // 2, dev)
        elif f == 1:
            send(bl, ha.at[1 - e], 8, dev)
        else:
            send(bf, hb.at[1 - e], 9, dev)

    for i in (2, 3):
        load[i].wait()
    done(rcv, 0, s1.at[pl.ds(0, 15)])

    zero = jnp.zeros((8, 128), F32)
    whole = low_forward(lambda t, ri: r1[t, ri])
    part = low_forward(lambda t, ri: zero if ri else r1[t, 0])
    y = y_forward(whole, part, lambda k: fh[k], lambda k: fl[k], off)
    for t in range(32):
        s2[t] = y[8 * t : 8 * t + 8]
    for d in u_order():
        t, dev = u_peer(d)
        send(s2.at[t], r2.at[u], 1, dev)
    r2[pl.ds(u, 1)] = s2[pl.ds(u, 1)]

    for i in range(4, 15):
        load[i].wait()
    for c in own:
        c.wait()
    done(rcv, 4, sp.at[pl.ds(0, 3), pl.ds(0, 2)])

    @pl.when(z == 0)
    def _():
        done(rcv, 5, sp.at[pl.ds(0, 3), 0])

    packed = jnp.where(z == 0, 2, 0)
    for zq in range(4):
        for alt in range(2):
            src = (packed if (zq >= 2) != (alt == 1) else 0, 1)
            for k0 in range(4):
                for pos in range(4):
                    k2 = POS_OF_K2.index(pos)
                    for j in range(2):
                        r = k0 * 8 + pos * 2 + j
                        bm[zq, alt, r : r + 1, :] = sp[
                            zq, src[j], k0 : k0 + 1, k2 * 128 : k2 * 128 + 128
                        ]
    sm = spread_spectrum(lambda zq, alt: bm[zq, alt], pick[...])

    done(rcv, 1, s2.at[pl.ds(0, 31)])

    def rows8(ref):
        return lambda i: ref[8 * i : 8 * i + 8, :]

    xh, xl = split(x_input(lambda t: r2[t], rows8(t1c), rows8(t1s)))
    q = dot3(gh[...], gl[...], xh, xl, NN)
    ws = []
    for k1 in range(32):
        a = slice(8 * k1, 8 * k1 + 8)
        c1, c2 = coefficients(sm[a, :128], sm[a, 128:], off, off_u)
        ws.append(x_middle(q[a], k1, t2c[a, :], t2s[a, :], c1, c2))
    xh, xl = split(jnp.concatenate(ws, axis=0))
    o = dot3(gth[...], gtl[...], xh, xl, NN)
    for t in range(32):
        a = slice(8 * t, 8 * t + 8)
        s3[t] = twist(o[a], t1c[a, :], -t1s[a, :])
    for d in u_order():
        t, dev = u_peer(d)
        send(s3.at[t], r3.at[u], 2, dev)
    r3[pl.ds(u, 1)] = s3[pl.ds(u, 1)]
    done(rcv, 2, s3.at[pl.ds(0, 31)])

    v = jnp.concatenate([r3[t] for t in range(32)], axis=0)
    first_part, second_part = y_backward(v, lambda k: fh[k], lambda k: fl[k], off)
    blocks = merge_planes(first_part, second_part, off)
    for t in range(16):
        for ri in range(2):
            s4[t, ri] = blocks[t][ri]
    for d in z_order():
        t, dev = z_peer(d)
        send(s4.at[t], r4.at[z], 3, dev)
    r4[pl.ds(z, 1)] = s4[pl.ds(z, 1)]

    first[3].wait()
    first[4].wait()
    for k in range(6):
        half = nbr_s[4 * k : 4 * k + 4, :]
        nd[k, 0:4, :] = half
        nd[k, 4:8, :] = half
    done(rcv, 6, hp.at[0])
    done(rcv, 7, hp.at[0])
    done(rcv, 8, ha)
    done(rcv, 9, hb)

    def plane(d, i):
        a = slice(8 * i, 8 * i + 8)
        return ms[a, :] if d == 1 else hp[d // 2, a, :]

    low = iota((8, 128), 0) < 4

    def edge(ref):
        def get(d, i):
            pair = ref[d, 2 * i : 2 * i + 2, :]
            return jnp.where(
                low,
                jnp.broadcast_to(pair[0:1], (8, 128)),
                jnp.broadcast_to(pair[1:2], (8, 128)),
            )

        return get

    def near_at(k, p, i):
        r = ((k * 8 + p) * 4 + i) * 8
        return near_s[r : r + 8, :]

    near_sum = near_of(plane, edge(ha), edge(hb), lambda k: nd[k], near_at)

    done(rcv, 3, s4.at[pl.ds(0, 15)])

    rt = jnp.concatenate([r4[t, ri] for t in range(16) for ri in range(2)], axis=0).T
    th, tl = split(rt)
    xs_h, xs_l = [], []
    for tx in range(4):
        mk = jnp.where(((lane16 >> 1) & 3) == tx, 1.0, 0.0).astype(BF16)
        mk = jnp.concatenate([jnp.concatenate([mk, mk], axis=1)] * 8, axis=0)
        xs_h.append(th * mk)
        xs_l.append(tl * mk)
    o = dot3(jnp.concatenate(xs_h, axis=0), jnp.concatenate(xs_l, axis=0), wxh[...], wxl[...], NN)

    def o_at(tx, r8, a, tz):
        r = tx * 128 + r8 * 16 + a * 8
        return o[r : r + 8, tz * 128 : tz * 128 + 128]

    far = far_of(proj_at, ungroup(z_backward_fold(o_at)))
    row = iota((8, 128), 0)
    both = cc[...]
    for i in range(4):
        a, b = far[2 * i] + near_sum[2 * i], far[2 * i + 1] + near_sum[2 * i + 1]
        tot = jnp.where(low, a + sub4(a), b + sub4(b))
        out[8 * i : 8 * i + 8, :] = jnp.where(2 * i + (row >> 2) < both, tot, 0.0)

    done(snd, 0, s1.at[pl.ds(0, 15)])
    done(snd, 1, s2.at[pl.ds(0, 31)])
    done(snd, 2, s3.at[pl.ds(0, 31)])
    done(snd, 3, s4.at[pl.ds(0, 15)])
    done(snd, 4, sp.at[pl.ds(0, 3), pl.ds(0, 2)])

    for d in (2, 1, 3):

        @pl.when(((zh + d) % 4) * 4 + zl == 0)
        def _():
            done(snd, 5, sp.at[0, 0])

    done(snd, 6, ms)
    done(snd, 7, ms)
    done(snd, 8, ha)
    done(snd, 9, hb)


def per_device(charges, counts, projection, near_blocks, neighbours, spectrum):
    tabs = [jnp.asarray(t) for t in tables()]
    ins = [
        charges.reshape(32, 128),
        counts.reshape(4, 128),
        projection.reshape(2048, 128),
        near_blocks.reshape(1536, 128),
        neighbours.reshape(24, 128),
        jnp.transpose(spectrum, (1, 2, 0)),
    ]
    vm = pltpu.VMEM
    scratch = [vm(t.shape, t.dtype) for t in tabs]
    scratch += [vm(a.shape, a.dtype) for a in ins[:5]]
    scratch += [
        vm((4, 3, 4, 512), F32),
        vm((4, 2, 32, 128), F32),
        vm((6, 8, 128), jnp.int32),
        vm((512, 512), BF16),
        vm((512, 512), BF16),
    ]
    scratch += [vm((16, 2, 8, 128), F32)] * 2 + [vm((32, 8, 128), F32)] * 4
    scratch += [vm((16, 2, 8, 128), F32)] * 2
    scratch += [
        vm((32, 128), F32),
        vm((8, 128), F32),
        vm((8, 128), F32),
        vm((2, 32, 128), F32),
        vm((3, 8, 128), F32),
        vm((3, 8, 128), F32),
        vm((8, 128), jnp.int32),
    ]
    dma = pltpu.SemaphoreType.DMA
    scratch += [dma((5,)), dma((15,)), dma((3,)), dma((10,)), dma((10,))]
    res = pl.pallas_call(
        body,
        out_shape=jax.ShapeDtypeStruct((32, 128), F32),
        in_specs=[pl.BlockSpec(memory_space=pl.ANY)] * (6 + len(tabs)),
        out_specs=pl.BlockSpec(memory_space=pltpu.VMEM),
        scratch_shapes=scratch,
        compiler_params=pltpu.CompilerParams(
            collective_id=0, has_side_effects=True, vmem_limit_bytes=48 << 20
        ),
        name="potential",
    )(*ins, *tabs)
    return res.reshape(8, 1, 512)


def solution(mesh):
    in_specs = (
        P(None, "slab", "cell"),
        P("slab", "cell"),
        P(None, None, "slab", "cell"),
        P(None, None, None, "slab", "cell"),
        P(None, "slab", "cell"),
        P(None, None, "slab"),
    )
    return jax.shard_map(
        per_device, mesh=mesh, in_specs=in_specs, out_specs=P(None, "slab", "cell"), check_vma=False
    )
```

time: 232 us -> 68.9 us (0.30); the launches traced: 228 us -> 68.2 us
  local copies, waits for them, and re-layouts: 83.6 us -> 19.9 us
  starting transfers between devices: 54.5 us -> 0 us
  Pallas kernels: 0 us -> 48.2 us
  waiting for transfers between devices: 43 us -> 0 us
  matrix products: 35.4 us -> 0 us
  other arithmetic: 10.2 us -> 0 us
    pallas_call x0 -> x1, Pallas kernels: none -> 48.2 us  [per_device(): pl.pallas_call(body, out_shape=jax.ShapeDtypeStruct((32, 128), F32), in_s...]
    all_to_all x4 -> x0, waiting for transfers between devices: 43 us -> none  [the longest x1 24.2 us: per_device(): lax.all_to_all(pencils, 'slab', split_axis=3, concat_axis=0, tiled=True)]
    all_to_all x4 -> x0, starting transfers between devices: 35.1 us -> none  [the longest x1 16.5 us: per_device(): lax.all_to_all(pencils, 'slab', split_axis=3, concat_axis=0, tiled=True)]
    dot_general x10 -> x0, matrix products: 32.9 us -> none  [the longest x2 14.9 us: transform_rows(): jnp.dot(flat_rows, sine_tab, precision=lax.Precision.HIGHEST)]
    another operation x5 -> x0, local copies, waits for them, and re-layouts: 22.1 us -> none  [the longest x2 18.5 us: per_device(): returned_x.reshape(columns.shape)]
    ppermute x4 -> x0, starting transfers between devices: 19.5 us -> none  [the longest x2 13.4 us: padded(): after = lax.ppermute(first, axis, down)]
    gather x4 -> x0, local copies, waits for them, and re-layouts: 11.7 us -> none  [the longest x1 10.9 us: per_device(): jnp.take(flat_ext, near_ids.reshape(-1), axis=1)]
    transpose x3 -> x0, local copies, waits for them, and re-layouts: 11.4 us -> none  [the longest x1 5.49 us: per_device(): tile_potential = grid_potential.reshape(cell_planes, TX, NZC, TZ, rows_ce...]
  transfers between devices with their start and end apart: 8 -> 0, of which waited for: 2 -> 0; matrix products, arithmetic and copies ran while one was open for 43% -> 0% of each run, Pallas kernels for 0% -> 0%
where the time goes in v1:
time: 68.9 us; the launch traced here: 68.2 us
  Pallas kernels  48.2 us (70%)
  local copies, waits for them, and re-layouts  19.9 us (29%)
    pallas_call x1, Pallas kernels, per_device(): pl.pallas_call(body, out_shape=jax.ShapeDtypeStruct((32, 128), F32), in_s...  48.2 us
    unnamed x43, local copies, waits for them, and re-layouts  19.9 us

profile of v1, /device:TPU:32, one launch (start us, length us, event | category | flops | bytes accessed | tf_op | source)
XLA Modules:
  0.0 68.2 jit_solution(14785690358589614235)
XLA Ops:
  0.0 0.0 copy-start.20
  0.0 0.7 copy-done.20
  0.7 0.0 copy-start
  0.7 1.2 %copy-done = f32[8,64,1,512]{3,2,1,0:T(1,128)S(1)} copy-done((f32[8,64,1,512]{3,2,1,0:T(1,128)S(1)}, f32[8,64,1,512]{3,2,1,0:T(1,128)}, u32[]{:S(2)}) %copy-start) | copy-done | bytes 1048600
  1.9 0.0 copy-start.1
  1.9 1.1 %copy-done.1 = f32[6,8,8,1,512]{4,3,2,1,0:T(1,128)S(1)} copy-done((f32[6,8,8,1,512]{4,3,2,1,0:T(1,128)S(1)}, f32[6,8,8,1,512]{4,3,2,1,0:T(1,128)}, u32[]{:S(2)}) %copy-start.1) | copy-done | bytes 786456
  3.0 0.0 copy-start.2
  3.0 1.0 %copy-done.2 = f32[512,64,4]{0,2,1:T(4,128)S(1)} copy-done((f32[512,64,4]{0,2,1:T(4,128)S(1)}, f32[512,64,4]{0,2,1:T(4,128)}, u32[]{:S(2)}) %copy-start.2) | copy-done | bytes 524312
  4.1 0.0 copy-start.3
  4.1 1.0 %copy-done.3 = bf16[4,256,256]{2,1,0:T(8,128)(2,1)S(1)} copy-done((bf16[4,256,256]{2,1,0:T(8,128)(2,1)S(1)}, bf16[4,256,256]{2,1,0:T(8,128)(2,1)}, u32[]{:S(2)}) %copy-start.3) | copy-done | bytes 524312
  5.1 0.0 copy-start.4
  5.1 1.0 %copy-done.4 = bf16[4,256,256]{2,1,0:T(8,128)(2,1)S(1)} copy-done((bf16[4,256,256]{2,1,0:T(8,128)(2,1)S(1)}, bf16[4,256,256]{2,1,0:T(8,128)(2,1)}, u32[]{:S(2)}) %copy-start.4) | copy-done | bytes 524312
  6.2 0.0 copy-start.5
  6.2 0.9 %copy-done.5 = bf16[256,512]{1,0:T(8,128)(2,1)S(1)} copy-done((bf16[256,512]{1,0:T(8,128)(2,1)S(1)}, bf16[256,512]{1,0:T(8,128)(2,1)}, u32[]{:S(2)}) %copy-start.5) | copy-done | bytes 262168
  7.1 0.0 copy-start.6
  7.1 0.9 %copy-done.6 = bf16[256,512]{1,0:T(8,128)(2,1)S(1)} copy-done((bf16[256,512]{1,0:T(8,128)(2,1)S(1)}, bf16[256,512]{1,0:T(8,128)(2,1)}, u32[]{:S(2)}) %copy-start.6) | copy-done | bytes 262168
  8.1 0.0 copy-start.7
  8.1 0.9 %copy-done.7 = bf16[256,512]{1,0:T(8,128)(2,1)S(1)} copy-done((bf16[256,512]{1,0:T(8,128)(2,1)S(1)}, bf16[256,512]{1,0:T(8,128)(2,1)}, u32[]{:S(2)}) %copy-start.7) | copy-done | bytes 262168
  9.0 0.0 copy-start.8
  9.0 0.9 %copy-done.8 = f32[256,128]{1,0:T(8,128)S(1)} copy-done((f32[256,128]{1,0:T(8,128)S(1)}, f32[256,128]{1,0:T(8,128)}, u32[]{:S(2)}) %copy-start.8) | copy-done | bytes 131096
  9.9 0.0 copy-start.9
  9.9 0.9 %copy-done.9 = f32[256,128]{1,0:T(8,128)S(1)} copy-done((f32[256,128]{1,0:T(8,128)S(1)}, f32[256,128]{1,0:T(8,128)}, u32[]{:S(2)}) %copy-start.9) | copy-done | bytes 131096
  10.8 0.0 copy-start.10
  10.8 0.9 %copy-done.10 = f32[256,128]{1,0:T(8,128)S(1)} copy-done((f32[256,128]{1,0:T(8,128)S(1)}, f32[256,128]{1,0:T(8,128)}, u32[]{:S(2)}) %copy-start.10) | copy-done | bytes 131096
  11.7 0.0 copy-start.11
  11.7 0.9 %copy-done.11 = f32[256,128]{1,0:T(8,128)S(1)} copy-done((f32[256,128]{1,0:T(8,128)S(1)}, f32[256,128]{1,0:T(8,128)}, u32[]{:S(2)}) %copy-start.11) | copy-done | bytes 131096
  12.6 0.0 copy-start.12
  12.6 0.9 %copy-done.12 = bf16[256,256]{1,0:T(8,128)(2,1)S(1)} copy-done((bf16[256,256]{1,0:T(8,128)(2,1)S(1)}, bf16[256,256]{1,0:T(8,128)(2,1)}, u32[]{:S(2)}) %copy-start.12) | copy-done | bytes 131096
  13.5 0.0 copy-start.13
  13.5 0.9 %copy-done.13 = bf16[256,256]{1,0:T(8,128)(2,1)S(1)} copy-done((bf16[256,256]{1,0:T(8,128)(2,1)S(1)}, bf16[256,256]{1,0:T(8,128)(2,1)}, u32[]{:S(2)}) %copy-start.13) | copy-done | bytes 131096
  14.4 0.0 copy-start.14
  14.4 0.9 %copy-done.14 = bf16[256,256]{1,0:T(8,128)(2,1)S(1)} copy-done((bf16[256,256]{1,0:T(8,128)(2,1)S(1)}, bf16[256,256]{1,0:T(8,128)(2,1)}, u32[]{:S(2)}) %copy-start.14) | copy-done | bytes 131096
  15.4 0.0 copy-start.15
  15.4 0.9 %copy-done.15 = bf16[256,256]{1,0:T(8,128)(2,1)S(1)} copy-done((bf16[256,256]{1,0:T(8,128)(2,1)S(1)}, bf16[256,256]{1,0:T(8,128)(2,1)}, u32[]{:S(2)}) %copy-start.15) | copy-done | bytes 131096
  16.3 0.0 copy-start.16
  16.3 0.8 %copy-done.16 = bf16[64,512]{1,0:T(8,128)(2,1)S(1)} copy-done((bf16[64,512]{1,0:T(8,128)(2,1)S(1)}, bf16[64,512]{1,0:T(8,128)(2,1)}, u32[]{:S(2)}) %copy-start.16) | copy-done | bytes 65560
  17.1 0.0 copy-start.17
  17.1 0.8 %copy-done.17 = bf16[64,512]{1,0:T(8,128)(2,1)S(1)} copy-done((bf16[64,512]{1,0:T(8,128)(2,1)S(1)}, bf16[64,512]{1,0:T(8,128)(2,1)}, u32[]{:S(2)}) %copy-start.17) | copy-done | bytes 65560
  17.9 0.0 copy-start.18
  17.9 0.7 %copy-done.18 = f32[8,1,512]{2,1,0:T(1,128)S(1)} copy-done((f32[8,1,512]{2,1,0:T(1,128)S(1)}, f32[8,1,512]{2,1,0:T(1,128)}, u32[]{:S(2)}) %copy-start.18) | copy-done | bytes 16408
  18.7 0.0 copy-start.19
  18.7 0.7 %copy-done.19 = s32[6,1,512]{2,1,0:T(1,128)S(1)} copy-done((s32[6,1,512]{2,1,0:T(1,128)S(1)}, s32[6,1,512]{2,1,0:T(1,128)}, u32[]{:S(2)}) %copy-start.19) | copy-done | bytes 12312
  19.4 48.2 %potential.1 = f32[32,128]{1,0:T(8,128)S(1)} custom-call(f32[32,128]{1,0:T(8,128)S(1)} %bitcast.11, s32[4,128]{1,0:T(4,128)S(1)} %bitcast.13, f32[2048,128]{1,0:T(8,128)S(1)} %bitcast.7, f32[1536,128]{1,0:T(8,128)S(1)} %bitcast.8, s32[24,128]{1,0:T(8,128)S(1)} %bitcast.12, f32[64,4,512]{2,1,0:T(4,128)S(1)} %bitcast.9, bf16[64,512]{1,0:T(8,128)(2,1)S(1)} %copy-done.17, ...), custom_call_target="tpu_custom_call" | custom-call | tf_op jit(solution)/shard_map/potential/pallas_call | solution.py:760
  67.5 0.6 copy.24
Async XLA Ops:
  0.0 0.7 %copy-start.20 = (s32[1,512]{1,0:T(1,128)S(1)}, s32[1,512]{1,0:T(1,128)}, u32[]{:S(2)}) copy-start(s32[1,512]{1,0:T(1,128)} %param.22) | copy-start | bytes 6148
  0.7 1.2 %copy-start = (f32[8,64,1,512]{3,2,1,0:T(1,128)S(1)}, f32[8,64,1,512]{3,2,1,0:T(1,128)}, u32[]{:S(2)}) copy-start(f32[8,64,1,512]{3,2,1,0:T(1,128)} %param.23) | copy-start | bytes 3145732
  1.9 1.1 %copy-start.1 = (f32[6,8,8,1,512]{4,3,2,1,0:T(1,128)S(1)}, f32[6,8,8,1,512]{4,3,2,1,0:T(1,128)}, u32[]{:S(2)}) copy-start(f32[6,8,8,1,512]{4,3,2,1,0:T(1,128)} %param.24) | copy-start | bytes 2359300
  3.0 1.0 %copy-start.2 = (f32[512,64,4]{0,2,1:T(4,128)S(1)}, f32[512,64,4]{0,2,1:T(4,128)}, u32[]{:S(2)}) copy-start(f32[512,64,4]{0,2,1:T(4,128)} %param.26) | copy-start | bytes 1572868
  4.1 1.0 %copy-start.3 = (bf16[4,256,256]{2,1,0:T(8,128)(2,1)S(1)}, bf16[4,256,256]{2,1,0:T(8,128)(2,1)}, u32[]{:S(2)}) copy-start(bf16[4,256,256]{2,1,0:T(8,128)(2,1)} %constant.33.clone.rest_3_) | copy-start | bytes 1572868
  5.1 1.0 %copy-start.4 = (bf16[4,256,256]{2,1,0:T(8,128)(2,1)S(1)}, bf16[4,256,256]{2,1,0:T(8,128)(2,1)}, u32[]{:S(2)}) copy-start(bf16[4,256,256]{2,1,0:T(8,128)(2,1)} %constant.32.clone.rest_2_) | copy-start | bytes 1572868
  6.2 0.9 %copy-start.5 = (bf16[256,512]{1,0:T(8,128)(2,1)S(1)}, bf16[256,512]{1,0:T(8,128)(2,1)}, u32[]{:S(2)}) copy-start(bf16[256,512]{1,0:T(8,128)(2,1)} %constant.44.clone.rest_14_) | copy-start | bytes 786436
  7.1 0.9 %copy-start.6 = (bf16[256,512]{1,0:T(8,128)(2,1)S(1)}, bf16[256,512]{1,0:T(8,128)(2,1)}, u32[]{:S(2)}) copy-start(bf16[256,512]{1,0:T(8,128)(2,1)} %constant.43.clone.rest_13_) | copy-start | bytes 786436
  8.1 0.9 %copy-start.7 = (bf16[256,512]{1,0:T(8,128)(2,1)S(1)}, bf16[256,512]{1,0:T(8,128)(2,1)}, u32[]{:S(2)}) copy-start(bf16[256,512]{1,0:T(8,128)(2,1)} %constant.42.clone.rest_12_) | copy-start | bytes 786436
  9.0 0.9 %copy-start.8 = (f32[256,128]{1,0:T(8,128)S(1)}, f32[256,128]{1,0:T(8,128)}, u32[]{:S(2)}) copy-start(f32[256,128]{1,0:T(8,128)} %constant.41.clone.rest_11_) | copy-start | bytes 393220
  9.9 0.9 %copy-start.9 = (f32[256,128]{1,0:T(8,128)S(1)}, f32[256,128]{1,0:T(8,128)}, u32[]{:S(2)}) copy-start(f32[256,128]{1,0:T(8,128)} %constant.40.clone.rest_10_) | copy-start | bytes 393220
  10.8 0.9 %copy-start.10 = (f32[256,128]{1,0:T(8,128)S(1)}, f32[256,128]{1,0:T(8,128)}, u32[]{:S(2)}) copy-start(f32[256,128]{1,0:T(8,128)} %constant.39.clone.rest_9_) | copy-start | bytes 393220
  11.7 0.9 %copy-start.11 = (f32[256,128]{1,0:T(8,128)S(1)}, f32[256,128]{1,0:T(8,128)}, u32[]{:S(2)}) copy-start(f32[256,128]{1,0:T(8,128)} %constant.38.clone.rest_8_) | copy-start | bytes 393220
  12.6 0.9 %copy-start.12 = (bf16[256,256]{1,0:T(8,128)(2,1)S(1)}, bf16[256,256]{1,0:T(8,128)(2,1)}, u32[]{:S(2)}) copy-start(bf16[256,256]{1,0:T(8,128)(2,1)} %constant.37.clone.rest_7_) | copy-start | bytes 393220
  13.5 0.9 %copy-start.13 = (bf16[256,256]{1,0:T(8,128)(2,1)S(1)}, bf16[256,256]{1,0:T(8,128)(2,1)}, u32[]{:S(2)}) copy-start(bf16[256,256]{1,0:T(8,128)(2,1)} %constant.36.clone.rest_6_) | copy-start | bytes 393220
  14.4 0.9 %copy-start.14 = (bf16[256,256]{1,0:T(8,128)(2,1)S(1)}, bf16[256,256]{1,0:T(8,128)(2,1)}, u32[]{:S(2)}) copy-start(bf16[256,256]{1,0:T(8,128)(2,1)} %constant.35.clone.rest_5_) | copy-start | bytes 393220
  15.4 0.9 %copy-start.15 = (bf16[256,256]{1,0:T(8,128)(2,1)S(1)}, bf16[256,256]{1,0:T(8,128)(2,1)}, u32[]{:S(2)}) copy-start(bf16[256,256]{1,0:T(8,128)(2,1)} %constant.34.clone.rest_4_) | copy-start | bytes 393220
  16.3 0.8 %copy-start.16 = (bf16[64,512]{1,0:T(8,128)(2,1)S(1)}, bf16[64,512]{1,0:T(8,128)(2,1)}, u32[]{:S(2)}) copy-start(bf16[64,512]{1,0:T(8,128)(2,1)} %constant.31.clone.rest_1_) | copy-start | bytes 196612
  17.1 0.8 %copy-start.17 = (bf16[64,512]{1,0:T(8,128)(2,1)S(1)}, bf16[64,512]{1,0:T(8,128)(2,1)}, u32[]{:S(2)}) copy-start(bf16[64,512]{1,0:T(8,128)(2,1)} %constant.30.clone.rest_0_) | copy-start | bytes 196612
  17.9 0.7 %copy-start.18 = (f32[8,1,512]{2,1,0:T(1,128)S(1)}, f32[8,1,512]{2,1,0:T(1,128)}, u32[]{:S(2)}) copy-start(f32[8,1,512]{2,1,0:T(1,128)} %param.21) | copy-start | bytes 49156
  18.7 0.7 %copy-start.19 = (s32[6,1,512]{2,1,0:T(1,128)S(1)}, s32[6,1,512]{2,1,0:T(1,128)}, u32[]{:S(2)}) copy-start(s32[6,1,512]{2,1,0:T(1,128)} %param.25) | copy-start | bytes 36868

commit v2 on v1

--- a/solution.py
+++ b/solution.py
@@ -763,9 +763,7 @@
         in_specs=[pl.BlockSpec(memory_space=pl.ANY)] * (6 + len(tabs)),
         out_specs=pl.BlockSpec(memory_space=pltpu.VMEM),
         scratch_shapes=scratch,
-        compiler_params=pltpu.CompilerParams(
-            collective_id=0, has_side_effects=True, vmem_limit_bytes=48 << 20
-        ),
+        compiler_params=pltpu.CompilerParams(collective_id=0, has_side_effects=True),
         name="potential",
     )(*ins, *tabs)
     return res.reshape(8, 1, 512)

time: 68.9 us -> 50.1 us (0.73)
  local copies, waits for them, and re-layouts: 19.9 us -> 1.32 us
    unnamed x43 -> x1, local copies, waits for them, and re-layouts: 19.9 us -> 1.32 us
where the time goes in v2:
time: 50.1 us; the launch traced here: 49.9 us
  Pallas kernels  48.5 us (97%)
  local copies, waits for them, and re-layouts  1.32 us (3%)
    pallas_call x1, Pallas kernels, per_device(): pl.pallas_call(body, out_shape=jax.ShapeDtypeStruct((32, 128), F32), in_s...  48.5 us
    unnamed x1, local copies, waits for them, and re-layouts  1.32 us

profile of v2, /device:TPU:32, one launch (start us, length us, event | category | flops | bytes accessed | tf_op | source)
XLA Modules:
  0.0 49.9 jit_solution(6665063933861241857)
XLA Ops:
  0.0 48.5 %potential.1 = f32[32,128]{1,0:T(8,128)} custom-call(f32[32,128]{1,0:T(8,128)} %bitcast.11, s32[4,128]{1,0:T(4,128)} %bitcast.13, f32[2048,128]{1,0:T(8,128)} %bitcast.7, f32[1536,128]{1,0:T(8,128)} %bitcast.8, s32[24,128]{1,0:T(8,128)} %bitcast.12, f32[64,4,512]{2,1,0:T(4,128)} %bitcast.9, bf16[64,512]{1,0:T(8,128)(2,1)} %constant.30.clone.rest_0_, ...), custom_call_target="tpu_custom_call" | custom-call | tf_op jit(solution)/shard_map/potential/pallas_call | solution.py:760
  48.5 1.3 %copy.24 = f32[8,1,512]{2,1,0:T(1,128)} copy(f32[8,1,512]{2,1,0:T(1,128)} %bitcast.10) | data formatting | bytes 32768

commit v3 on v2

--- a/solution.py
+++ b/solution.py
@@ -453,8 +453,8 @@
     (ch_s, cnt_s, proj_s, near_s, nbr_s) = scr[15:20]
     (sp, bm, nd, tp_h, tp_l) = scr[20:25]
     (s1, r1, s2, r2, s3, r3, s4, r4) = scr[25:33]
-    (ms, bf, bl, hp, ha, hb, cc) = scr[33:40]
-    (in_sem, tab_sem, loc_sem, snd, rcv) = scr[40:]
+    (ms, bf, bl, hp, ha, hb, cc, rb, rs) = scr[33:42]
+    (in_sem, tab_sem, loc_sem, snd, rcv, rsem) = scr[42:]
     (wzh, wzl, fh, fl, gh, gl, gth, gtl, t1c, t1s, t2c, t2s, pick, wxh, wxl) = tab
 
     slab, zl = lax.axis_index("slab"), lax.axis_index("cell")
@@ -464,9 +464,12 @@
     off = z
     off_u = u
 
+    def z_dev(t):
+        return ((t // 4) * NU + u, t % 4)
+
     def z_peer(d):
-        t = (z + d) % 16
-        return t, ((t // 4) * NU + u, t % 4)
+        t = (z + d + 16) % 16
+        return t, z_dev(t)
 
     def u_peer(d):
         t = ((u // 8 + d[0]) % 4) * 8 + ((u // 2 % 4 + d[1]) % 4) * 2 + (u + d[2]) % 2
@@ -488,8 +491,7 @@
         c.start()
 
     barrier = pltpu.get_barrier_semaphore()
-    peers = [z_peer(d)[1] for d in z_order()] + [u_peer(d)[1] for d in u_order()]
-    peers += [near_peer(e, f) for e, f in halo]
+    peers = [z_peer(d)[1] for d in (12, 4, 13, 3, 14, 2, 15, 1)] + [u_peer(d)[1] for d in u_order()]
     for p in peers:
         pl.semaphore_signal(barrier, inc=1, device_id=p, device_id_type=pl.DeviceIdType.MESH)
     for c in load[2:] + first[3:]:
@@ -500,12 +502,12 @@
     for c in own:
         c.start()
 
-    def send(src, dst, i, dev):
+    def send(src, dst, i, dev, arrival=None):
         pltpu.make_async_remote_copy(
             src_ref=src,
             dst_ref=dst,
             send_sem=snd.at[i],
-            recv_sem=rcv.at[i],
+            recv_sem=rcv.at[i] if arrival is None else arrival,
             device_id=dev,
             device_id_type=pl.DeviceIdType.MESH,
         ).start()
@@ -550,30 +552,51 @@
                 r = t * 4 + ri * 2
                 s1[t, ri, 2 * tx : 2 * tx + 2, :] = o[r : r + 2, tx * 128 : tx * 128 + 128]
     pl.semaphore_wait(barrier, len(peers))
-    for d in z_order():
+
+    core = u % 2
+    opp_in, opp_out = (z + 12 + 8 * core) % 16, (z + 4 + 8 * core) % 16
+    relays = []
+    for m in (3, 2, 1):
+        for side, sgn in ((0, 1), (1, -1)):
+            relays.append((side * 3 + m - 1, (z + 16 + sgn * (4 + m)) % 16, z_peer(4 * sgn)[1], z_peer(-4 * sgn)[0], z_peer(m * sgn)[1]))
+    opp = (6, (z + 8) % 16, z_dev(opp_out), opp_in, z_dev(opp_out))
+    relays = [opp] + relays
+    for slot, t, dev, _, _ in relays:
+        send(s1.at[t], rb.at[slot], 0, dev, rsem.at[slot])
+    for d in (4, 12, 3, 13, 2, 14, 1, 15):
         t, dev = z_peer(d)
         send(s1.at[t], r1.at[z], 0, dev)
     r1[pl.ds(z, 1)] = s1[pl.ds(z, 1)]
 
-    for d in (2, 1, 3):
-        th = (zh + d) % 4
-        dev = (th * NU + u, zl)
-        tz_id = th * 4 + zl
+    far_id = (z + 8) % 16
+    for j in range(2):
+        send(spec.at[far_id + 16 * j], rs.at[j], 4, z_dev(opp_out), rsem.at[7 + j])
+
+    @pl.when(far_id == 0)
+    def _():
+        send(spec.at[far_id + 32], rs.at[2], 5, z_dev(opp_out), rsem.at[9])
+
+    for slot, _, _, src, dev in relays:
+        done(rsem, slot, rb.at[slot])
+        send(rb.at[slot], r1.at[src], 10, dev, rcv.at[0])
+
+    for d in (4, 12):
+        t, dev = z_peer(d)
         for j in range(2):
-            send(spec.at[tz_id + 16 * j], sp.at[zh, j], 4, dev)
-
-        @pl.when(tz_id == 0)
+            send(spec.at[t + 16 * j], sp.at[zh, j], 4, dev)
+
+        @pl.when(t == 0)
         def _():
-            send(spec.at[tz_id + 32], sp.at[zh, 2], 5, dev)
-
-    for e, f in halo:
-        dev = near_peer(e, f)
-        if f == 0:
-            send(ms, hp.at[(1 - e) // 2], 6 + (1 - e) // 2, dev)
-        elif f == 1:
-            send(bl, ha.at[1 - e], 8, dev)
-        else:
-            send(bf, hb.at[1 - e], 9, dev)
+            send(spec.at[t + 32], sp.at[zh, 2], 5, dev)
+
+    for j in range(2):
+        done(rsem, 7 + j, rs.at[j])
+        send(rs.at[j], sp.at[opp_in // 4, j], 11, z_dev(opp_out), rcv.at[4])
+
+    @pl.when(opp_out == 0)
+    def _():
+        done(rsem, 9, rs.at[2])
+        send(rs.at[2], sp.at[opp_in // 4, 2], 12, z_dev(opp_out), rcv.at[5])
 
     for i in (2, 3):
         load[i].wait()
@@ -635,6 +658,15 @@
         t, dev = u_peer(d)
         send(s3.at[t], r3.at[u], 2, dev)
     r3[pl.ds(u, 1)] = s3[pl.ds(u, 1)]
+
+    for e, f in halo:
+        dev = near_peer(e, f)
+        if f == 0:
+            send(ms, hp.at[(1 - e) // 2], 6 + (1 - e) // 2, dev)
+        elif f == 1:
+            send(bl, ha.at[1 - e], 8, dev)
+        else:
+            send(bf, hb.at[1 - e], 9, dev)
     done(rcv, 2, s3.at[pl.ds(0, 31)])
 
     v = jnp.concatenate([r3[t] for t in range(32)], axis=0)
@@ -712,11 +744,18 @@
     done(snd, 3, s4.at[pl.ds(0, 15)])
     done(snd, 4, sp.at[pl.ds(0, 3), pl.ds(0, 2)])
 
-    for d in (2, 1, 3):
-
-        @pl.when(((zh + d) % 4) * 4 + zl == 0)
+    for t in ((z + 8) % 16, (z + 4) % 16, (z + 12) % 16):
+
+        @pl.when(t == 0)
         def _():
             done(snd, 5, sp.at[0, 0])
+
+    @pl.when(opp_out == 0)
+    def _():
+        done(snd, 12, sp.at[0, 0])
+
+    done(snd, 10, s1.at[pl.ds(0, 7)])
+    done(snd, 11, rs.at[pl.ds(0, 2)])
 
     done(snd, 6, ms)
     done(snd, 7, ms)
@@ -754,9 +793,11 @@
         vm((3, 8, 128), F32),
         vm((3, 8, 128), F32),
         vm((8, 128), jnp.int32),
+        vm((7, 2, 8, 128), F32),
+        vm((3, 4, 512), F32),
     ]
     dma = pltpu.SemaphoreType.DMA
-    scratch += [dma((5,)), dma((15,)), dma((3,)), dma((10,)), dma((10,))]
+    scratch += [dma((5,)), dma((15,)), dma((3,)), dma((13,)), dma((10,)), dma((10,))]
     res = pl.pallas_call(
         body,
         out_shape=jax.ShapeDtypeStruct((32, 128), F32),

time: 50.1 us -> 49.7 us (level)
  the two profiles are of different devices: /device:TPU:32 before, /device:TPU:1 now
where the time goes in v3:
time: 49.7 us; the launch traced here: 49.4 us
  Pallas kernels  48.1 us (97%)
  local copies, waits for them, and re-layouts  1.32 us (3%)
    pallas_call x1, Pallas kernels, per_device(): pl.pallas_call(body, out_shape=jax.ShapeDtypeStruct((32, 128), F32), in_s...  48.1 us
    unnamed x1, local copies, waits for them, and re-layouts  1.32 us

profile of v3, /device:TPU:1, one launch (start us, length us, event | category | flops | bytes accessed | tf_op | source)
XLA Modules:
  0.0 49.4 jit_solution(16322190871430215426)
XLA Ops:
  0.0 48.1 %potential.1 = f32[32,128]{1,0:T(8,128)} custom-call(f32[32,128]{1,0:T(8,128)} %bitcast.11, s32[4,128]{1,0:T(4,128)} %bitcast.13, f32[2048,128]{1,0:T(8,128)} %bitcast.7, f32[1536,128]{1,0:T(8,128)} %bitcast.8, s32[24,128]{1,0:T(8,128)} %bitcast.12, f32[64,4,512]{2,1,0:T(4,128)} %bitcast.9, bf16[64,512]{1,0:T(8,128)(2,1)} %constant.30.clone.rest_0_, ...), custom_call_target="tpu_custom_call" | custom-call | tf_op jit(solution)/shard_map/potential/pallas_call | solution.py:801
  48.1 1.3 %copy.24 = f32[8,1,512]{2,1,0:T(1,128)} copy(f32[8,1,512]{2,1,0:T(1,128)} %bitcast.10) | data formatting | bytes 32768

commit v4 on v3

--- a/solution.py
+++ b/solution.py
@@ -247,20 +247,15 @@
 def y_forward(whole, part, fh, fl, off):
     rows = []
     for k0 in range(4):
-        x = jnp.concatenate(
-            [
-                jnp.concatenate([jnp.concatenate(y[k0], axis=0) for y in pair], axis=1)
-                for pair in (whole, part)
-            ],
-            axis=0,
-        )
-        xh, xl = split(x)
+        pairs = (whole,) if part is None else (whole, part)
+        x = [jnp.concatenate([jnp.concatenate(y[k0], axis=0) for y in pair], axis=1) for pair in pairs]
+        xh, xl = split(jnp.concatenate(x, axis=0))
         o = dot3(xh, xl, fh(k0), fl(k0), NT)
-        rows.append(y_fixup(o[:32], o[32:], k0, off))
+        rows.append(o if part is None else y_fixup(o[:32], o[32:], k0, off))
     return jnp.concatenate(rows, axis=0).T
 
 
-def y_backward(v, fh, fl, off):
+def y_backward(v, fh, fl, off, packed=True):
     vt = v.T
     first, second = ([], []), ([], [])
     for k0 in range(4):
@@ -273,9 +268,9 @@
         vb = jnp.where(zq >= 2, a, 0.0)
         if k0 == 0:
             vb = jnp.where(alone, jnp.where(ri == 0, roll(a, -4, 1), -roll(a, 4, 1)), vb)
-        xh, xl = split(jnp.concatenate([va, vb], axis=0))
+        xh, xl = split(jnp.concatenate([va, vb], axis=0) if packed else a)
         o = dot3(xh, xl, fh(k0), fl(k0), NN)
-        for half, pair in enumerate((first, second)):
+        for half, pair in enumerate((first, second) if packed else (first,)):
             for ri_part in range(2):
                 pair[ri_part].append(
                     [
@@ -305,8 +300,11 @@
 
 
 def merge_planes(first, second, off):
+    a = low_backward(first)
+    if second is None:
+        return [a[z // 4][z % 4] for z in range(16)]
     special = (iota((8, 128), 0) & 1) + off == 0
-    a, b = low_backward(first), low_backward(second)
+    b = low_backward(second)
     return [
         (a[z // 4][z % 4][0], jnp.where(special, b[z // 4][z % 4][0], a[z // 4][z % 4][1]))
         for z in range(16)
@@ -318,24 +316,14 @@
 
 
 def x_input(r2, tc, ts):
+    return jnp.concatenate([twist(r2(u), tc(u), ts(u)) for u in range(32)], axis=0)
+
+
+def conjugate(v):
     lane, row = iota((8, 128), 1), iota((8, 128), 0)
     kx0 = (lane >> 3) & 3
-    main, conj = [], []
-    for u in range(32):
-        v = r2(u)
-        w = jnp.where(kx0 == 1, roll(v, -16, 1), jnp.where(kx0 == 3, roll(v, 16, 1), v))
-        w = jnp.where(row < 4, w, -w)
-        main.append(twist(v, tc(u), ts(u)))
-        conj.append(twist(w, tc(u), ts(u)))
-    return jnp.concatenate(
-        [jnp.concatenate(main, axis=0), jnp.concatenate(conj, axis=0)], axis=1
-    )
-
-
-def x_middle(q, k1, tc, ts, c1, c2):
-    a = lane_dft4(twist(q[:, :128], tc, ts), -1)
-    b = lane_dft4(twist(q[:, 128:], tc, ts), -1)
-    return twist(lane_dft4(a * c1 + b * c2, 1), tc, -ts)
+    w = jnp.where(kx0 == 1, roll(v, -16, 1), jnp.where(kx0 == 3, roll(v, 16, 1), v))
+    return jnp.where(row < 4, w, -w)
 
 
 def coefficients(sm, sa, off, off_u):
@@ -454,7 +442,8 @@
     (sp, bm, nd, tp_h, tp_l) = scr[20:25]
     (s1, r1, s2, r2, s3, r3, s4, r4) = scr[25:33]
     (ms, bf, bl, hp, ha, hb, cc, rb, rs) = scr[33:42]
-    (in_sem, tab_sem, loc_sem, snd, rcv, rsem) = scr[42:]
+    (k_main, k_conj, extra) = scr[42:45]
+    (in_sem, tab_sem, loc_sem, snd, rcv, rsem) = scr[45:]
     (wzh, wzl, fh, fl, gh, gl, gth, gtl, t1c, t1s, t2c, t2s, pick, wxh, wxl) = tab
 
     slab, zl = lax.axis_index("slab"), lax.axis_index("cell")
@@ -557,14 +546,14 @@
     opp_in, opp_out = (z + 12 + 8 * core) % 16, (z + 4 + 8 * core) % 16
     relays = []
     for m in (3, 2, 1):
-        for side, sgn in ((0, 1), (1, -1)):
+        for side, sgn in ((0, 1 - 2 * core), (1, 2 * core - 1)):
             relays.append((side * 3 + m - 1, (z + 16 + sgn * (4 + m)) % 16, z_peer(4 * sgn)[1], z_peer(-4 * sgn)[0], z_peer(m * sgn)[1]))
     opp = (6, (z + 8) % 16, z_dev(opp_out), opp_in, z_dev(opp_out))
     relays = [opp] + relays
     for slot, t, dev, _, _ in relays:
         send(s1.at[t], rb.at[slot], 0, dev, rsem.at[slot])
     for d in (4, 12, 3, 13, 2, 14, 1, 15):
-        t, dev = z_peer(d)
+        t, dev = z_peer(d + core * (16 - 2 * d))
         send(s1.at[t], r1.at[z], 0, dev)
     r1[pl.ds(z, 1)] = s1[pl.ds(z, 1)]
 
@@ -603,11 +592,16 @@
     done(rcv, 0, s1.at[pl.ds(0, 15)])
 
     zero = jnp.zeros((8, 128), F32)
-    whole = low_forward(lambda t, ri: r1[t, ri])
-    part = low_forward(lambda t, ri: zero if ri else r1[t, 0])
-    y = y_forward(whole, part, lambda k: fh[k], lambda k: fl[k], off)
-    for t in range(32):
-        s2[t] = y[8 * t : 8 * t + 8]
+
+    def y_stage(packed):
+        whole = low_forward(lambda t, ri: r1[t, ri])
+        part = low_forward(lambda t, ri: zero if ri else r1[t, 0]) if packed else None
+        y = y_forward(whole, part, lambda k: fh[k], lambda k: fl[k], off)
+        for t in range(32):
+            s2[t] = y[8 * t : 8 * t + 8]
+
+    pl.when(z == 0)(lambda: y_stage(True))
+    pl.when(z != 0)(lambda: y_stage(False))
     for d in u_order():
         t, dev = u_peer(d)
         send(s2.at[t], r2.at[u], 1, dev)
@@ -636,19 +630,37 @@
                             zq, src[j], k0 : k0 + 1, k2 * 128 : k2 * 128 + 128
                         ]
     sm = spread_spectrum(lambda zq, alt: bm[zq, alt], pick[...])
-
-    done(rcv, 1, s2.at[pl.ds(0, 31)])
-
-    def rows8(ref):
-        return lambda i: ref[8 * i : 8 * i + 8, :]
-
-    xh, xl = split(x_input(lambda t: r2[t], rows8(t1c), rows8(t1s)))
-    q = dot3(gh[...], gl[...], xh, xl, NN)
-    ws = []
     for k1 in range(32):
         a = slice(8 * k1, 8 * k1 + 8)
         c1, c2 = coefficients(sm[a, :128], sm[a, 128:], off, off_u)
-        ws.append(x_middle(q[a], k1, t2c[a, :], t2s[a, :], c1, c2))
+        k_main[k1] = c1
+        k_conj[k1] = c2
+        extra[k1] = zero
+
+    done(rcv, 1, s2.at[pl.ds(0, 31)])
+
+    def rows8(ref):
+        return lambda i: ref[8 * i : 8 * i + 8, :]
+
+    def x_forward(r):
+        xh, xl = split(x_input(r, rows8(t1c), rows8(t1s)))
+        q = dot3(gh[...], gl[...], xh, xl, NN)
+        out = []
+        for k1 in range(32):
+            a = slice(8 * k1, 8 * k1 + 8)
+            out.append(lane_dft4(twist(q[a], t2c[a, :], t2s[a, :]), -1))
+        return out
+
+    @pl.when(z + u == 0)
+    def _():
+        for k1, b in enumerate(x_forward(lambda t: conjugate(r2[t]))):
+            extra[k1] = b * k_conj[k1]
+
+    ws = []
+    for k1, b in enumerate(x_forward(lambda t: r2[t])):
+        a = slice(8 * k1, 8 * k1 + 8)
+        w = lane_dft4(b * k_main[k1] + extra[k1], 1)
+        ws.append(twist(w, t2c[a, :], -t2s[a, :]))
     xh, xl = split(jnp.concatenate(ws, axis=0))
     o = dot3(gth[...], gtl[...], xh, xl, NN)
     for t in range(32):
@@ -669,14 +681,19 @@
             send(bf, hb.at[1 - e], 9, dev)
     done(rcv, 2, s3.at[pl.ds(0, 31)])
 
-    v = jnp.concatenate([r3[t] for t in range(32)], axis=0)
-    first_part, second_part = y_backward(v, lambda k: fh[k], lambda k: fl[k], off)
-    blocks = merge_planes(first_part, second_part, off)
-    for t in range(16):
-        for ri in range(2):
-            s4[t, ri] = blocks[t][ri]
+
+    def y_back_stage(packed):
+        v = jnp.concatenate([r3[t] for t in range(32)], axis=0)
+        a, b = y_backward(v, lambda k: fh[k], lambda k: fl[k], off, packed)
+        blocks = merge_planes(a, b if packed else None, off)
+        for t in range(16):
+            for ri in range(2):
+                s4[t, ri] = blocks[t][ri]
+
+    pl.when(z == 0)(lambda: y_back_stage(True))
+    pl.when(z != 0)(lambda: y_back_stage(False))
     for d in z_order():
-        t, dev = z_peer(d)
+        t, dev = z_peer(d + core * (16 - 2 * d))
         send(s4.at[t], r4.at[z], 3, dev)
     r4[pl.ds(z, 1)] = s4[pl.ds(z, 1)]
 
@@ -796,6 +813,7 @@
         vm((7, 2, 8, 128), F32),
         vm((3, 4, 512), F32),
     ]
+    scratch += [vm((32, 8, 128), F32)] * 3
     dma = pltpu.SemaphoreType.DMA
     scratch += [dma((5,)), dma((15,)), dma((3,)), dma((13,)), dma((10,)), dma((10,))]
     res = pl.pallas_call(

time: 49.7 us -> 49.3 us (level)
  the two profiles are of different devices: /device:TPU:1 before, /device:TPU:32 now
where the time goes in v4:
time: 49.3 us; the launch traced here: 49 us
  Pallas kernels  47.7 us (97%)
  local copies, waits for them, and re-layouts  1.32 us (3%)
    pallas_call x1, Pallas kernels, per_device(): pl.pallas_call(body, out_shape=jax.ShapeDtypeStruct((32, 128), F32), in_s...  47.7 us
    unnamed x1, local copies, waits for them, and re-layouts  1.32 us

profile of v4, /device:TPU:32, one launch (start us, length us, event | category | flops | bytes accessed | tf_op | source)
XLA Modules:
  0.0 49.0 jit_solution(1446948453951404673)
XLA Ops:
  0.0 47.7 %potential.1 = f32[32,128]{1,0:T(8,128)} custom-call(f32[32,128]{1,0:T(8,128)} %bitcast.11, s32[4,128]{1,0:T(4,128)} %bitcast.13, f32[2048,128]{1,0:T(8,128)} %bitcast.7, f32[1536,128]{1,0:T(8,128)} %bitcast.8, s32[24,128]{1,0:T(8,128)} %bitcast.12, f32[64,4,512]{2,1,0:T(4,128)} %bitcast.9, bf16[64,512]{1,0:T(8,128)(2,1)} %constant.30.clone.rest_0_, ...), custom_call_target="tpu_custom_call" | custom-call | tf_op jit(solution)/shard_map/potential/pallas_call | solution.py:819
  47.7 1.3 %copy.24 = f32[8,1,512]{2,1,0:T(1,128)} copy(f32[8,1,512]{2,1,0:T(1,128)} %bitcast.10) | data formatting | bytes 32768

commit v5 on v4

--- a/solution.py
+++ b/solution.py
@@ -461,7 +461,8 @@
         return t, z_dev(t)
 
     def u_peer(d):
-        t = ((u // 8 + d[0]) % 4) * 8 + ((u // 2 % 4 + d[1]) % 4) * 2 + (u + d[2]) % 2
+        side = 1 + 2 * (u % 2)
+        t = ((u // 8 + side * d[0]) % 4) * 8 + ((u // 2 % 4 + side * d[1]) % 4) * 2 + (u + d[2]) % 2
         return t, (zh * NU + t, zl)
 
     def near_peer(e, f):

time: 49.3 us -> 49.3 us (level)
  no operation moved by 1% of the time
where the time goes in v5:
time: 49.3 us; the launch traced here: 49 us
  Pallas kernels  47.7 us (97%)
  local copies, waits for them, and re-layouts  1.32 us (3%)
    pallas_call x1, Pallas kernels, per_device(): pl.pallas_call(body, out_shape=jax.ShapeDtypeStruct((32, 128), F32), in_s...  47.7 us
    unnamed x1, local copies, waits for them, and re-layouts  1.32 us

profile of v5, /device:TPU:32, one launch (start us, length us, event | category | flops | bytes accessed | tf_op | source)
XLA Modules:
  0.0 49.0 jit_solution(5490935039621418302)
XLA Ops:
  0.0 47.7 %potential.1 = f32[32,128]{1,0:T(8,128)} custom-call(f32[32,128]{1,0:T(8,128)} %bitcast.11, s32[4,128]{1,0:T(4,128)} %bitcast.13, f32[2048,128]{1,0:T(8,128)} %bitcast.7, f32[1536,128]{1,0:T(8,128)} %bitcast.8, s32[24,128]{1,0:T(8,128)} %bitcast.12, f32[64,4,512]{2,1,0:T(4,128)} %bitcast.9, bf16[64,512]{1,0:T(8,128)(2,1)} %constant.30.clone.rest_0_, ...), custom_call_target="tpu_custom_call" | custom-call | tf_op jit(solution)/shard_map/potential/pallas_call | solution.py:820
  47.7 1.3 %copy.24 = f32[8,1,512]{2,1,0:T(1,128)} copy(f32[8,1,512]{2,1,0:T(1,128)} %bitcast.10) | data formatting | bytes 32768
